TPU v7x, 128 devices: a whole 4x4x4 slice. The times are simulated.
128 devices in a mesh: lat: 16 (over z, y), lon: 8 (over x, core).
Axes of the slice: x: 4, y: 4, z: 4, core: 2. Of those that a mesh axis runs over, the one named last changes fastest.
Arguments:
- encoder_features: bfloat16 [512, 256, 128], P('lat', 'lon'), may hold values from -6 to 6
- noise: bfloat16 [512, 256, 128], P('lat', 'lon'), may hold values from -6 to 6
- patch_cols: int32 [16, 32], P('lat'), may hold values from 0 to 255, as said below
- timesteps: int32 [16, 32], P('lat'), may hold values from 0 to 31
- w_conv: bfloat16 [1152, 128], replicated, may hold values from -0.1875 to 0.1875
- w_down: bfloat16 [512, 256], replicated, may hold values from -0.25 to 0.25
- w_up: bfloat16 [256, 512], replicated, may hold values from -0.375 to 0.375
- w_out: bfloat16 [128, 128], replicated, may hold values from -0.5 to 0.5
Outputs:
- feature_grad: float32 [512, 256, 128], P('lat', 'lon')
- grad_conv: float32 [1152, 128], replicated
- grad_down: float32 [512, 256], replicated
- grad_up: float32 [256, 512], replicated
- grad_out: float32 [128, 128], replicated
- loss_value: float32 [], replicated
Inputs may be any that keep to these rules, and one draw needn't show every extreme that they name: `patch_cols`: in each band at most 12 patches start in one device's block of 32 longitude cells, and exactly 12 start in one block.
All inputs are finite; a program needn't handle non-finite values.
Results may differ from a plain program's by a relative error of at most 0.009.
Values may be sent and summed in bfloat16 or wider, within the bound.
No kernel may reach another device: no remote copies, remote signals or barrier semaphores. Data moves between devices by JAX's collectives and lax.ppermute only.
A program may use at most 64 MiB of HBM per device.

v0:
```python
import math

import jax
import jax.numpy as jnp
from jax import lax
from jax.sharding import PartitionSpec as P

NSTEPS = 32
PMAX = 12


sigma_low = 0.02
sigma_high = 20.0


def shifted(block, axis, distance):
    devices = range(lax.axis_size(axis))
    route = [((i - distance) % len(devices), i) for i in devices]
    return lax.ppermute(block, axis, route)


def sigma_of(levels):
    return sigma_low * jnp.exp(
        levels.astype(jnp.float32) / (NSTEPS - 1) * math.log(sigma_high / sigma_low)
    )


def patch_loss(feat, noise_patch, sigma, w_conv, w_down, w_up, w_out):
    side = feat.shape[0]
    chans = feat.shape[2]
    scale_in = 1.0 / jnp.sqrt(1.0 + sigma * sigma)
    hidden = (scale_in * (feat + sigma * noise_patch.astype(jnp.float32))).astype(jnp.bfloat16)
    padded = jnp.pad(hidden, ((1, 1), (1, 1), (0, 0)))
    stacked = jnp.concatenate(
        [
            padded[row_off : row_off + side, col_off : col_off + side]
            for row_off in range(3)
            for col_off in range(3)
        ],
        axis=-1,
    ).reshape(side * side, 9 * chans)
    first = jax.nn.silu(jnp.dot(stacked, w_conv, preferred_element_type=jnp.float32)).astype(
        jnp.bfloat16
    )
    coarse_in = (
        first.reshape(side // 2, 2, side // 2, 2, chans)
        .transpose(0, 2, 1, 3, 4)
        .reshape(side * side // 4, 4 * chans)
    )
    coarse = jax.nn.silu(jnp.dot(coarse_in, w_down, preferred_element_type=jnp.float32)).astype(
        jnp.bfloat16
    )
    upward = (
        jnp.dot(coarse, w_up, preferred_element_type=jnp.float32)
        .reshape(side // 2, side // 2, 2, 2, chans)
        .transpose(0, 2, 1, 3, 4)
        .reshape(side * side, chans)
    )
    merged = (first.astype(jnp.float32) + upward).astype(jnp.bfloat16)
    predicted = jnp.dot(merged, w_out, preferred_element_type=jnp.float32)
    error = predicted - noise_patch.reshape(side * side, chans).astype(jnp.float32)
    return jnp.sum(error * error) / (2.0 * chans)


def patch_grads(window_feat, window_noise, start, sigma, weights, live):
    side = window_feat.shape[0]
    feat = lax.dynamic_slice_in_dim(window_feat, start, side, 1).astype(jnp.float32)
    noise_patch = lax.dynamic_slice_in_dim(window_noise, start, side, 1)

    def local_loss(feat_in, conv_in, down_in, up_in, out_in):
        return patch_loss(feat_in, noise_patch, sigma, conv_in, down_in, up_in, out_in)

    value, pull = jax.vjp(local_loss, feat, *weights)
    return (value * live, pull(live))


def run_slots(window_feat, window_noise, starts, sigmas, lives, weights):
    side = window_feat.shape[0]

    def one_slot(inner, slot):
        grad_win, sums = inner
        start = starts[slot]
        value, grads = patch_grads(
            window_feat, window_noise, start, sigmas[slot], weights, lives[slot]
        )
        current = lax.dynamic_slice_in_dim(grad_win, start, side, 1)
        grad_win = lax.dynamic_update_slice_in_dim(grad_win, current + grads[0], start, 1)
        sums = tuple(
            (total + part.astype(jnp.float32) for total, part in zip(sums[:4], grads[1:]))
        ) + (sums[4] + value,)
        return ((grad_win, sums), None)

    empty = jnp.zeros(window_feat.shape, jnp.float32)
    init = tuple((jnp.zeros(w.shape, jnp.float32) for w in weights)) + (jnp.zeros((), jnp.float32),)
    (grad_win, sums), unused = lax.scan(
        one_slot, (empty, init), jnp.arange(starts.shape[0], dtype=jnp.int32)
    )
    return (grad_win, sums)


def per_device(encoder_features, noise, patch_cols, timesteps, w_conv, w_down, w_up, w_out):
    weights = (w_conv, w_down, w_up, w_out)
    side = encoder_features.shape[0]
    block_cols = encoder_features.shape[1]
    lon_index = lax.axis_index("lon")
    band_starts = patch_cols[0]
    band_levels = timesteps[0]
    band_patches = band_starts.shape[0]
    neighbor = shifted((encoder_features, noise), "lon", -1)
    window_feat = jnp.concatenate([encoder_features, neighbor[0]], axis=1)
    window_noise = jnp.concatenate([noise, neighbor[1]], axis=1)
    owners = band_starts // block_cols
    is_mine = owners == lon_index
    positions = jnp.arange(band_patches, dtype=jnp.int32)
    sort_key = jnp.where(is_mine, 0, band_patches) + positions
    picked = jnp.argsort(sort_key)[:PMAX]
    lives = is_mine[picked].astype(jnp.float32)
    starts = jnp.clip(band_starts[picked] - lon_index * block_cols, 0, block_cols)
    grad_win, sums = run_slots(
        window_feat, window_noise, starts, sigma_of(band_levels[picked]), lives, weights
    )
    returned = shifted(grad_win[:, block_cols:].astype(jnp.bfloat16), "lon", 1).astype(jnp.float32)
    feature_grad = grad_win[:, :block_cols] + returned
    totals = lax.psum((sums[0], sums[1], sums[2], sums[3], sums[4]), ("lat", "lon"))
    loss_value = totals[4] / (lax.axis_size("lat") * band_patches * side * side)
    return (feature_grad, totals[0], totals[1], totals[2], totals[3], loss_value)


def solution(mesh):
    placed = (
        P("lat", "lon", None),
        P("lat", "lon", None),
        P("lat", None),
        P("lat", None),
        P(),
        P(),
        P(),
        P(),
    )
    return jax.shard_map(
        per_device,
        mesh=mesh,
        in_specs=placed,
        out_specs=(P("lat", "lon", None), P(), P(), P(), P(), P()),
        check_vma=False,
    )
```

profile of v0, /device:TPU:1, one launch (start us, length us, event | category | flops | bytes accessed | tf_op | source)
XLA Modules:
  0.0 558.3 jit_solution(14067091899618015423)
XLA Ops:
  8.7 2.3 collective-permute-start.1
  18.9 372.6 %while.23 = (s32[]{:T(128)}, f32[32,64,128]{2,1,0:T(8,128)S(1)}, f32[1152,128]{1,0:T(8,128)}, f32[512,256]{1,0:T(8,128)S(1)}, f32[256,512]{1,0:T(8,128)}, /*inde...) while((s32[]{:T(128)}, f32[32,64,128]{2,1,0:T(8,128)S(1)}, ...), condition=%wide.region_3.4_spmd.clone, body=%wide.region_1.3_spmd.clone.sunk | while | flops 1422756864 | bytes 64128688 | solution.py:95
  36.5 2.0 fusion.115
  40.8 2.9 fusion.113
  43.7 2.0 convolution_convert_fusion.11
  67.3 2.2 fusion.115
  71.8 2.9 fusion.113
  74.7 2.0 convolution_convert_fusion.11
  98.4 2.2 fusion.115
  102.9 2.9 fusion.113
  129.4 2.2 fusion.115
  133.9 2.9 fusion.113
  136.8 2.0 convolution_convert_fusion.11
  160.5 2.2 fusion.115
  165.0 2.9 fusion.113
  167.9 2.0 convolution_convert_fusion.11
  191.6 2.2 fusion.115
  196.1 2.9 fusion.113
  222.6 2.2 fusion.115
  227.2 2.9 fusion.113
  253.7 2.2 fusion.115
  258.2 2.9 fusion.113
  284.8 2.2 fusion.115
  289.3 2.9 fusion.113
  315.8 2.2 fusion.115
  320.3 2.9 fusion.113
  346.9 2.2 fusion.115
  351.4 2.9 fusion.113
  378.0 2.2 fusion.115
  382.5 2.9 fusion.113
  392.3 69.1 %psum.39 = f32[]{:T(128)} all-reduce(f32[]{:T(128)} %get-tuple-element.593), channel_id=1, replica_groups=mesh['lat'=16,'lon'=8] {'lat','lon'}, use_global_device_ids=true, to_apply=%region_8.9 | all-reduce | flops 1 | bytes 8 | tf_op jit(solution)/shard_map/psum | solution.py:124
  463.0 82.1 %all-reduce.13.cloned.1.call-done = (f32[1152,128]{1,0:T(8,128)}, f32[512,256]{1,0:T(8,128)}, f32[256,512]{1,0:T(8,128)}, f32[128,128]{1,0:T(8,128)}) async-done(((f32[1152,128]{1,0:T(8,128)}, f32[512,256]{1,0:T(8,128)}, f32[256,512]{1,0:T(8,128)}, f32[128,128]{1,0:T(8,128)}), (f32[1152,128]{1,0:T(8,128)}, f32[512,256]{1,0:T(8,128)}, f32[256,512]{1,0:T(8,128)}, ...) | async-done | bytes 1703952 | tf_op jit(solution)/shard_map/psum | solution.py:124
  (684 shorter events, 231.2 us)
Async XLA Ops:
  7.2 6.1 %copy-start = (s32[1,32]{1,0:T(1,128)S(1)}, s32[1,32]{1,0:T(1,128)}, u32[]{:S(2)}) copy-start(s32[1,32]{1,0:T(1,128)} %param.13) | copy-start | bytes 388
  7.2 10.7 %copy-start.11 = (bf16[32,32,128]{2,1,0:T(8,128)(2,1)S(1)}, bf16[32,32,128]{2,1,0:T(8,128)(2,1)}, u32[]{:S(2)}) copy-start(bf16[32,32,128]{2,1,0:T(8,128)(2,1)} %param.11) | copy-start | bytes 786436
  7.2 537.9 %all-reduce.13.cloned.1.call-start = ((), (), s32[]{:S(2)}) async-start(), calls=%async_computation | async-start | bytes 3407872 | tf_op jit(solution)/shard_map/psum | solution.py:124
  7.2 8.8 %collective-permute-start = (bf16[32,32,128]{2,1,0:T(8,128)(2,1)}, bf16[32,32,128]{2,1,0:T(8,128)(2,1)S(1)}, u32[]{:S(2)}, u32[]{:S(2)}) collective-permute-start(bf16[32,32,128]{2,1,0:T(8,128)(2,1)} %param.10), channel_id=1, source_target_pairs={{1,0},{2,1},{3,2},{4,3},{5,4},{6,5},{7,6},{0,7},{9,8},{10,9},{11,1... | collective-permute-start | bytes 786440 | tf_op jit(solution)/shard_map/ppermute | solution.py:19
  8.7 9.2 %collective-permute-start.1 = (bf16[32,32,128]{2,1,0:T(8,128)(2,1)}, bf16[32,32,128]{2,1,0:T(8,128)(2,1)S(1)}, u32[]{:S(2)}, u32[]{:S(2)}) collective-permute-start(bf16[32,32,128]{2,1,0:T(8,128)(2,1)} %param.11), channel_id=1, source_target_pairs={{1,0},{2,1},{3,2},{4,3},{5,4},{6,5},{7,6},{0,7},{9,8},{10,9},{11,1... | collective-permute-start | bytes 786440 | tf_op jit(solution)/shard_map/ppermute | solution.py:19
  13.2 5.6 copy-start.1
  13.3 5.6 copy-start.5
  13.3 5.6 copy-start.13
  13.3 5.6 copy-start.15
  77.2 3.6 copy-start.14
  77.2 3.6 copy-start.16
  139.3 3.6 copy-start.14
  139.3 3.6 copy-start.16
  170.4 3.6 copy-start.14
  170.4 3.6 copy-start.16
  201.4 3.6 copy-start.14
  201.5 3.6 copy-start.16
  232.5 3.6 copy-start.14
  232.5 3.6 copy-start.16
  263.6 3.6 copy-start.14
  263.6 3.6 copy-start.16
  294.6 3.6 copy-start.14
  294.7 3.6 copy-start.16
  325.7 3.6 copy-start.14
  325.7 3.6 copy-start.16
  356.8 3.6 copy-start.14
  356.8 3.6 copy-start.16
  387.8 3.6 copy-start.14
  387.9 3.6 copy-start.16
  392.3 69.8 %collective-permute-start.2 = (bf16[32,32,128]{2,1,0:T(8,128)(2,1)S(1)}, bf16[32,32,128]{2,1,0:T(8,128)(2,1)S(1)}, u32[]{:S(2)}, u32[]{:S(2)}) collective-permute-start(bf16[32,32,128]{2,1,0:T(8,128)(2,1)S(1)} %slice.108), channel_id=1, source_target_pairs={{7,0},{0,1},{1,2},{2,3},{3,4},{4,5},{5,6},{6,7},{15,8},{8,9},{9,10... | collective-permute-start | bytes 786440 | tf_op jit(solution)/shard_map/ppermute | solution.py:19
  545.1 3.9 copy-start.10
  545.1 4.6 copy-start.12
  (78 other events, 153.8 us)
Sparse Core Ops, SparseCore 0:
  392.4 152.6 all-reduce.12
where the time goes:
time: 562 us; the launch traced here: 558 us
  matrix products  148 us (26%)
  local copies, waits for them, and re-layouts  98.1 us (17%)
  loops' own time  89.1 us (16%)
  waiting for transfers between devices  82.1 us (15%)
  blocking collectives  69.1 us (12%)
  other arithmetic  52.6 us (9%)
  between operations  16 us (3%)
    another operation x1, loops' own time, run_slots(): lax.scan(one_slot, (empty, init), jnp.arange(starts.shape[0], dtype=jnp.i...  89.1 us
    psum x1, waiting for transfers between devices, per_device(): lax.psum((sums[0], sums[1], sums[2], sums[3], sums[4]), ('lat', 'lon'))  82.1 us
    dot_general x36, matrix products, patch_loss(): jnp.dot(stacked, w_conv, preferred_element_type=jnp.float32)  77.3 us
    psum x1, blocking collectives, per_device(): lax.psum((sums[0], sums[1], sums[2], sums[3], sums[4]), ('lat', 'lon'))  69.1 us
    dot_general x36, matrix products, patch_loss(): jnp.dot(coarse, w_up, preferred_element_type=jnp.float32)  43.8 us
    convert_element_type x12, other arithmetic, patch_loss(): (scale_in * (feat + sigma * noise_patch.astype(jnp.float32))).astype(jnp....  23.5 us
    while x288, local copies, waits for them, and re-layouts  19.8 us
    dot_general x36, matrix products, patch_loss(): predicted = jnp.dot(merged, w_out, preferred_element_type=jnp.float32)  16.8 us
  transfers between devices with their start and end apart: 4, of which 1 were waited for; matrix products, arithmetic and copies ran while one was open for 1% of the time, Pallas kernels for 0%

commit v1 on v0

v1 whole, which is shorter than its diff:
```python
import math

import jax
import jax.numpy as jnp
from jax import lax
from jax.experimental import pallas as pl
from jax.experimental.pallas import tpu as pltpu
from jax.sharding import PartitionSpec as P

NSTEPS = 32
PMAX = 12
SIDE = 32
HALF = 16
C = 128
CELLS = SIDE * HALF
CHUNK = 32
NDEV = 128

sigma_low = 0.02
sigma_high = 20.0

bf16 = jnp.bfloat16
f32 = jnp.float32


def shifted(block, axis, distance):
    devices = range(lax.axis_size(axis))
    route = [((i - distance) % len(devices), i) for i in devices]
    return lax.ppermute(block, axis, route)


def sigma_of(levels):
    return sigma_low * jnp.exp(
        levels.astype(jnp.float32) / (NSTEPS - 1) * math.log(sigma_high / sigma_low)
    )


def dot(a, b):
    return jnp.dot(a, b, preferred_element_type=f32)


def dot_t(a, b):
    return lax.dot_general(a, b, (((0,), (0,)), ((), ())), preferred_element_type=f32)


def pack_rows(block):
    rows, cols, chans = block.shape
    return block.reshape(rows // 2, 2, cols, chans).transpose(2, 0, 1, 3).reshape(
        cols, rows // 2, 2 * chans
    )


def unpack_rows(block):
    cols, half, lanes = block.shape
    return block.reshape(cols, half, 2, lanes // 2).transpose(1, 2, 0, 3).reshape(
        2 * half, cols, lanes // 2
    )


def fill_slots(slots, value):
    row = lax.broadcasted_iota(jnp.int32, (CELLS, C), 0) % HALF
    even = value[:, :C]
    odd = value[:, C:]
    above = jnp.where(row == 0, 0.0, pltpu.roll(odd, 1, 0))
    below = jnp.where(row == HALF - 1, 0.0, pltpu.roll(even, CELLS - 1, 0))
    slots[1 : SIDE + 1, :, 0:C] = above.astype(bf16).reshape(SIDE, HALF, C)
    slots[1 : SIDE + 1, :, C : 3 * C] = value.astype(bf16).reshape(SIDE, HALF, 2 * C)
    slots[1 : SIDE + 1, :, 3 * C : 4 * C] = below.astype(bf16).reshape(SIDE, HALF, C)


def zero_edges(slots):
    slots[0] = jnp.zeros((HALF, 4 * C), bf16)
    slots[SIDE + 1] = jnp.zeros((HALF, 4 * C), bf16)


def taps(slots):
    return jnp.concatenate(
        [slots[d : d + SIDE].reshape(CELLS, 4 * C) for d in range(3)], axis=-1
    )


def patch_kernel(
    count, starts, alphas, betas,
    feat, noise, w_in, w_dn, w_dn_t, w_u, w_u_t, w_o, w_o_t,
    dpre_out, grads_out,
    slots, first, slope, g_conv, g_down, g_up, g_out, loss,
):
    g_conv[...] = jnp.zeros_like(g_conv)
    g_down[...] = jnp.zeros_like(g_down)
    g_up[...] = jnp.zeros_like(g_up)
    g_out[...] = jnp.zeros_like(g_out)
    loss[...] = jnp.zeros_like(loss)
    zero_edges(slots)

    def one_patch(k, carry):
        start = starts[k]
        f = feat[pl.ds(start, SIDE)].reshape(CELLS, 2 * C).astype(f32)
        e = noise[pl.ds(start, SIDE)].reshape(CELLS, 2 * C).astype(f32)
        fill_slots(slots, alphas[k] * f + betas[k] * e)
        pre = dot(taps(slots), w_in[...])
        sig = 0.5 * jnp.tanh(0.5 * pre) + 0.5
        act = pre * sig
        slope[...] = (sig + act * (1.0 - sig)).reshape(SLOPE)
        first[...] = act.astype(bf16).reshape(SLOPE)
        cells = jnp.concatenate([first[:, b].reshape(256, 256) for b in range(2)], axis=-1)
        pre2 = dot(cells, w_dn[...])
        sig2 = 0.5 * jnp.tanh(0.5 * pre2) + 0.5
        act2 = pre2 * sig2
        slope2 = sig2 + act2 * (1.0 - sig2)
        coarse = act2.astype(bf16)
        up = dot(coarse, w_u[...])
        ep = noise.at[pl.ds(start, SIDE)]
        merged = []
        dmerged = []
        derr = []
        for b in range(2):
            m = (first[:, b].reshape(256, 256).astype(f32) + up[:, 256 * b : 256 * b + 256]).astype(bf16)
            eps = ep[...].reshape(HALF, 2, HALF, 2 * C)[:, b].reshape(256, 256).astype(f32)
            err = dot(m, w_o[...]) - eps
            loss[...] += jnp.sum((err * err).reshape(32, 8, 256), axis=0)
            d = (err * (1.0 / C)).astype(bf16)
            merged.append(m)
            derr.append(d)
            dmerged.append(dot(d, w_o_t[...]).astype(bf16))
        g_out[...] += dot_t(jnp.concatenate(merged, axis=0), jnp.concatenate(derr, axis=0))
        dm = jnp.concatenate(dmerged, axis=-1)
        g_up[...] += dot_t(coarse, dm)
        dpre2 = (dot(dm, w_u_t[...]) * slope2).astype(bf16)
        g_down[...] += dot_t(dpre2, cells)
        dcells = dot(dpre2, w_dn_t[...])
        for b in range(2):
            df = dmerged[b].astype(f32) + dcells[:, 256 * b : 256 * b + 256]
            dp = df * slope[:, b].reshape(256, 256)
            first[:, b] = dp.astype(bf16).reshape(HALF, HALF, 2 * C)
        dpre = first[...].reshape(CELLS, 2 * C)
        dpre_out[k] = dpre
        g_conv[...] += dot_t(dpre, taps(slots))
        return carry

    lax.fori_loop(0, count[0], one_patch, 0)

    for i in range(3):
        for j in range(3):
            block = g_conv[0:C, pl.ds((4 * j + i) * C, C)] + g_conv[C:, pl.ds((4 * j + i + 1) * C, C)]
            grads_out[pl.ds((3 * i + j) * C, C)] = block.T.astype(bf16)
    base = 9 * C
    for a in range(2):
        for b in range(2):
            for h in range(2):
                block = g_down[h * C : h * C + C, (2 * b + a) * C : (2 * b + a + 1) * C]
                grads_out[pl.ds(base + ((2 * a + b) * 2 + h) * C, C)] = block.T.astype(bf16)
    base = 17 * C
    for a in range(2):
        for b in range(2):
            for h in range(2):
                block = g_up[h * C : h * C + C, (2 * b + a) * C : (2 * b + a + 1) * C]
                grads_out[pl.ds(base + ((2 * a + b) * 2 + h) * C, C)] = block.astype(bf16)
    base = 25 * C
    grads_out[pl.ds(base, C)] = (g_out[0:C, 0:C] + g_out[C:, C:]).astype(bf16)
    base = 26 * C
    part = jnp.sum(loss[:, 0:C] + loss[:, C:], axis=0, keepdims=True)
    high = part.astype(bf16)
    low = (part - high.astype(f32)).astype(bf16)
    row = lax.broadcasted_iota(jnp.int32, (C, C), 0)
    grads_out[pl.ds(base, C)] = jnp.where(
        row == 0, high.astype(f32), jnp.where(row == 1, low.astype(f32), 0.0)
    ).astype(bf16)
    grads_out[pl.ds(27 * C, 5 * C)] = jnp.zeros((5 * C, C), bf16)


SLOPE = (HALF, 2, HALF, 2 * C)


def input_kernel(count, starts, alphas, dpre, w_back, out, slots):
    out[...] = jnp.zeros_like(out)
    zero_edges(slots)

    def one_patch(k, carry):
        fill_slots(slots, dpre[k].astype(f32))
        back = dot(taps(slots), w_back[...]) * alphas[k]
        window = out.at[pl.ds(starts[k], SIDE)]
        window[...] += back.reshape(SIDE, HALF, 2 * C)
        return carry

    lax.fori_loop(0, count[0], one_patch, 0)


def smem():
    return pl.BlockSpec(memory_space=pltpu.SMEM)


def vmem():
    return pl.BlockSpec(memory_space=pltpu.VMEM)


def run_patches(count, starts, alphas, betas, feat, noise, weights):
    return pl.pallas_call(
        patch_kernel,
        out_shape=(
            jax.ShapeDtypeStruct((PMAX, CELLS, 2 * C), bf16),
            jax.ShapeDtypeStruct((NDEV * CHUNK, C), bf16),
        ),
        in_specs=[smem()] * 4 + [vmem()] * 9,
        out_specs=(vmem(), vmem()),
        scratch_shapes=[
            pltpu.VMEM((SIDE + 2, HALF, 4 * C), bf16),
            pltpu.VMEM(SLOPE, bf16),
            pltpu.VMEM(SLOPE, f32),
            pltpu.VMEM((2 * C, 12 * C), f32),
            pltpu.VMEM((2 * C, 4 * C), f32),
            pltpu.VMEM((2 * C, 4 * C), f32),
            pltpu.VMEM((2 * C, 2 * C), f32),
            pltpu.VMEM((8, 2 * C), f32),
        ],
        compiler_params=pltpu.CompilerParams(vmem_limit_bytes=50 << 20),
        name="patches",
    )(count, starts, alphas, betas, feat, noise, *weights)


def run_inputs(count, starts, alphas, dpre, w_back):
    return pl.pallas_call(
        input_kernel,
        out_shape=jax.ShapeDtypeStruct((2 * SIDE, HALF, 2 * C), f32),
        in_specs=[smem()] * 3 + [vmem()] * 2,
        out_specs=vmem(),
        scratch_shapes=[pltpu.VMEM((SIDE + 2, HALF, 4 * C), bf16)],
        compiler_params=pltpu.CompilerParams(vmem_limit_bytes=50 << 20),
        name="inputs",
    )(count, starts, alphas, dpre, w_back)


def layout_weights(w_conv, w_down, w_up, w_out):
    zero = jnp.zeros((C, C), bf16)
    conv = w_conv.reshape(3, 3, C, C)

    def fwd(dc, s, a):
        return conv[s - a, dc] if 0 <= s - a < 3 else zero

    def back(dc, s, p):
        return conv[p + 2 - s, 2 - dc].T if 0 <= p + 2 - s < 3 else zero

    def grid(block):
        return jnp.concatenate(
            [
                jnp.concatenate([block(dc, s, a) for a in range(2)], axis=1)
                for dc in range(3)
                for s in range(4)
            ],
            axis=0,
        )

    down = w_down.reshape(2, 2, C, 2 * C).transpose(1, 0, 2, 3).reshape(4 * C, 2 * C)
    up = w_up.reshape(2 * C, 2, 2, C).transpose(0, 2, 1, 3).reshape(2 * C, 4 * C)

    def twice(w):
        return jnp.concatenate(
            [jnp.concatenate([w, zero], axis=1), jnp.concatenate([zero, w], axis=1)], axis=0
        )

    return (grid(fwd), down, down.T, up, up.T, twice(w_out), twice(w_out.T)), grid(back)


def per_device(encoder_features, noise, patch_cols, timesteps, w_conv, w_down, w_up, w_out):
    block_cols = encoder_features.shape[1]
    lon_index = lax.axis_index("lon")
    starts_all = patch_cols[0]
    band_patches = starts_all.shape[0]

    both = jnp.stack([pack_rows(encoder_features), pack_rows(noise)])
    nxt = shifted(both, "lon", -1)
    window = jnp.concatenate([both, nxt], axis=1)

    mine = (starts_all // block_cols) == lon_index
    rank = jnp.cumsum(mine.astype(jnp.int32)) - 1
    pick = mine[None, :] & (rank[None, :] == jnp.arange(PMAX, dtype=jnp.int32)[:, None])
    starts = jnp.sum(jnp.where(pick, starts_all[None, :] - lon_index * block_cols, 0), axis=1)
    levels = jnp.sum(jnp.where(pick, timesteps[0][None, :], 0), axis=1)
    count = jnp.sum(mine.astype(jnp.int32)).reshape(1)
    sigma = sigma_of(levels)
    alphas = 1.0 / jnp.sqrt(1.0 + sigma * sigma)
    betas = alphas * sigma

    weights, w_back = layout_weights(w_conv, w_down, w_up, w_out)
    dpre, grads = run_patches(count, starts, alphas, betas, window[0], window[1], weights)

    chunks = lax.all_to_all(grads.reshape(NDEV, CHUNK, C), ("lat", "lon"), 0, 0, tiled=True)
    grad_win = run_inputs(count, starts, alphas, dpre, w_back)
    returned = shifted(grad_win[block_cols:].astype(bf16), "lon", 1)
    feature_grad = unpack_rows(grad_win[:block_cols] + returned.astype(f32))

    mean = jnp.sum(chunks.astype(f32), axis=0)
    high = mean.astype(bf16)
    total = mean[0:2].sum(axis=0)
    total_high = total.astype(bf16)
    total_low = (total - total_high.astype(f32)).astype(bf16)
    device = lax.axis_index("lat") * lax.axis_size("lon") + lon_index
    fixed = jnp.concatenate([total_high[None], total_low[None], high[2:]], axis=0)
    high = jnp.where(device == 26 * C // CHUNK, fixed, high)
    sums = lax.all_to_all(
        jnp.broadcast_to(high[None], (NDEV, CHUNK, C)), ("lat", "lon"), 0, 0, tiled=True
    ).reshape(NDEV * CHUNK, C)

    grad_conv = sums[: 9 * C].astype(f32)
    grad_down = (
        sums[9 * C : 17 * C].astype(f32).reshape(4, 2, C, C).transpose(0, 2, 1, 3).reshape(4 * C, 2 * C)
    )
    grad_up = (
        sums[17 * C : 25 * C].astype(f32).reshape(4, 2, C, C).transpose(1, 2, 0, 3).reshape(2 * C, 4 * C)
    )
    grad_out = sums[25 * C : 26 * C].astype(f32)
    objective = jnp.sum(sums[26 * C : 26 * C + 2].astype(f32)) / (2.0 * C)
    side = encoder_features.shape[0]
    loss_value = objective / (lax.axis_size("lat") * band_patches * side * side)
    return (feature_grad, grad_conv, grad_down, grad_up, grad_out, loss_value)


def solution(mesh):
    placed = (
        P("lat", "lon", None),
        P("lat", "lon", None),
        P("lat", None),
        P("lat", None),
        P(),
        P(),
        P(),
        P(),
    )
    return jax.shard_map(
        per_device,
        mesh=mesh,
        in_specs=placed,
        out_specs=(P("lat", "lon", None), P(), P(), P(), P(), P()),
        check_vma=False,
    )
```

time: 562 us -> 112 us (0.20)
  matrix products: 148 us -> 0 us
  loops' own time: 89.1 us -> 0 us
  local copies, waits for them, and re-layouts: 98.1 us -> 10 us
  blocking collectives: 69.1 us -> 0 us
  other arithmetic: 52.6 us -> 3.69 us
  waiting for transfers between devices: 82.1 us -> 35.3 us
  starting transfers between devices: 3.77 us -> 43.1 us
  Pallas kernels: 0 us -> 16.1 us
  between operations: 16 us -> 2.95 us
    dot_general x144 -> x0, matrix products: 148 us -> none  [the longest x36 77.3 us: patch_loss(): jnp.dot(stacked, w_conv, preferred_element_type=jnp.float32)]
    another operation x1 -> x0, loops' own time: 89.1 us -> none  [run_slots(): lax.scan(one_slot, (empty, init), jnp.arange(starts.shape[0], dtype=jnp.i...]
    psum x1 -> x0, waiting for transfers between devices: 82.1 us -> none  [per_device(): lax.psum((sums[0], sums[1], sums[2], sums[3], sums[4]), ('lat', 'lon'))]
    psum x1 -> x0, blocking collectives: 69.1 us -> none  [per_device(): lax.psum((sums[0], sums[1], sums[2], sums[3], sums[4]), ('lat', 'lon'))]
    all_to_all x0 -> x2, starting transfers between devices: none -> 40.1 us  [the longest x1 35.7 us: per_device(): lax.all_to_all(grads.reshape(NDEV, CHUNK, C), ('lat', 'lon'), 0, 0, tiled...]
    convert_element_type x25 -> x5, other arithmetic: 36.3 us -> 1.53 us  [the longest x1 0.87 us: per_device(): grad_conv = sums[:9 * C].astype(f32)]
    dynamic_slice x48 -> x0, local copies, waits for them, and re-layouts: 28.8 us -> none  [the longest x12 7.64 us: one_slot(): lives[slot]]
    all_to_all x0 -> x2, waiting for transfers between devices: none -> 23.3 us  [the longest x1 19.2 us: per_device(): lax.all_to_all(grads.reshape(NDEV, CHUNK, C), ('lat', 'lon'), 0, 0, tiled...]
  transfers between devices with their start and end apart: 4 -> 4, of which waited for: 1 -> 4; matrix products, arithmetic and copies ran while one was open for 1% -> 5% of each run, Pallas kernels for 0% -> 4%
where the time goes in v1:
time: 112 us; the launch traced here: 111 us
  starting transfers between devices  43.1 us (38%)
  waiting for transfers between devices  35.3 us (32%)
  Pallas kernels  16.1 us (14%)
  local copies, waits for them, and re-layouts  10 us (9%)
  other arithmetic  3.69 us (3%)
  between operations  2.95 us (3%)
    all_to_all x1, starting transfers between devices, per_device(): lax.all_to_all(grads.reshape(NDEV, CHUNK, C), ('lat', 'lon'), 0, 0, tiled...  35.7 us
    all_to_all x1, waiting for transfers between devices, per_device(): lax.all_to_all(grads.reshape(NDEV, CHUNK, C), ('lat', 'lon'), 0, 0, tiled...  19.2 us
    ppermute x2, waiting for transfers between devices, shifted(): return lax.ppermute(block, axis, route)  11.9 us
    pallas_call x1, Pallas kernels, run_patches(): pl.pallas_call(patch_kernel, out_shape=(jax.ShapeDtypeStruct((PMAX, CELLS...  11.7 us
    pallas_call x1, Pallas kernels, run_inputs(): pl.pallas_call(input_kernel, out_shape=jax.ShapeDtypeStruct((2 * SIDE, HA...  4.41 us
    all_to_all x1, starting transfers between devices, per_device(): lax.all_to_all(jnp.broadcast_to(high[None], (NDEV, CHUNK, C)), ('lat', 'l...  4.33 us
    all_to_all x1, waiting for transfers between devices, per_device(): lax.all_to_all(jnp.broadcast_to(high[None], (NDEV, CHUNK, C)), ('lat', 'l...  4.14 us
    ppermute x2, starting transfers between devices, shifted(): return lax.ppermute(block, axis, route)  3.07 us
  transfers between devices with their start and end apart: 4, of which 4 were waited for; matrix products, arithmetic and copies ran while one was open for 5% of the time, Pallas kernels for 4%

profile of v1, /device:TPU:1, one launch (start us, length us, event | category | flops | bytes accessed | tf_op | source)
XLA Modules:
  0.0 111.2 jit_solution(9217419652288454350)
XLA Ops:
  0.6 1.2 %copy.86 = bf16[16,2,32,128]{3,1,0,2:T(2,128)(2,1)S(1)} copy(bf16[16,2,32,128]{3,2,1,0:T(8,128)(2,1)} %bitcast.155) | data formatting | bytes 524288 | tf_op jit(solution)/shard_map/reshape | solution.py:48
  1.8 0.2 stack_reshape.6
  2.1 1.2 %copy.85 = bf16[16,2,32,128]{3,1,0,2:T(2,128)(2,1)S(1)} copy(bf16[16,2,32,128]{3,2,1,0:T(8,128)(2,1)} %bitcast.156) | data formatting | bytes 524288 | tf_op jit(solution)/shard_map/reshape | solution.py:48
  3.3 0.2 stack_reshape.7
  3.5 1.4 %collective-permute-start = (bf16[2,32,16,256]{3,2,1,0:T(8,128)(2,1)S(1)}, bf16[2,32,16,256]{3,2,1,0:T(8,128)(2,1)S(1)}, u32[]{:S(2)}, u32[]{:S(2)}) collective-permute-start(bf16[2,32,16,256]{3,2,1,0:T(8,128)(2,1)S(1)} %constant_dynamic-update-slice_fusion), channel_id=1, source_target_pairs={{1,0},{2,1},{3,2},{4,3},{5,4},{6,5},{7,6},{0,7},{9,8},{10,9},{11,1... | collective-permute-start | bytes 1572872 | tf_op jit(solution)/shard_map/ppermute | solution.py:29
  6.2 0.1 copy.76
  6.4 0.3 copy.62.w_in
  7.0 0.2 copy.59
  7.3 0.1 copy.63.w_dn
  7.5 0.2 copy.60
  7.7 0.1 copy.64.w_u
  8.1 0.6 fusion.11
  8.7 4.2 %collective-permute-done = bf16[2,32,16,256]{3,2,1,0:T(8,128)(2,1)S(1)} collective-permute-done((bf16[2,32,16,256]{3,2,1,0:T(8,128)(2,1)S(1)}, bf16[2,32,16,256]{3,2,1,0:T(8,128)(2,1)S(1)}, u32[]{:S(2)}, u32[]{:S(2)}) %collective-permute-start) | collective-permute-done | bytes 524320 | tf_op jit(solution)/shard_map/ppermute | solution.py:29
  13.1 11.7 %patches.1 = (bf16[12,512,256]{2,1,0:T(8,128)(2,1)}, bf16[4096,128]{1,0:T(8,128)(2,1)}) custom-call(s32[1]{0:T(128)} %bitcast.1.count, s32[12]{0:T(128)S(1)} %get-tuple-element.11.starts, f32[12]{0:T(128)S(1)} %get-tuple-element.13.alphas, f32[12]{0:T(128)S(1)} %get-tuple-element.12.betas, bf16[64,16,256]{2,1,0:T(8,128)(2,1)S(1)} %get-tuple-element.19.feat, ...), custom_call_target="tpu_custom_call" | custom-call | tf_op jit(solution)/shard_map/patches/pallas_call | solution.py:197
  24.7 35.7 %all-to-all-start = ((bf16[128,32,128]{2,1,0:T(8,128)(2,1)}), bf16[128,32,128]{2,1,0:T(8,128)(2,1)S(1)}, u32[]{:S(2)}, u32[]{:S(2)}) async-start(bf16[128,32,128]{2,1,0:T(8,128)(2,1)} %bitcast.109), calls=%async_computation | async-start | bytes 2097152 | tf_op jit(solution)/shard_map/all_to_all | solution.py:286
  60.6 19.2 %all-to-all-done = bf16[128,32,128]{2,1,0:T(8,128)(2,1)S(1)} async-done(((bf16[128,32,128]{2,1,0:T(8,128)(2,1)}), bf16[128,32,128]{2,1,0:T(8,128)(2,1)S(1)}, u32[]{:S(2)}, u32[]{:S(2)}) %all-to-all-start) | async-done | bytes 1048608 | tf_op jit(solution)/shard_map/all_to_all | solution.py:286
  79.8 0.2 convert_reduce_fusion
  80.1 1.1 %broadcast_in_dim.39 = bf16[128,32,128]{2,1,0:T(8,128)(2,1)} broadcast(bf16[32,128]{1,0:T(8,128)(2,1)S(1)} %maximum_select_fusion), dimensions={1,2} | broadcast | bytes 1056768 | tf_op jit(solution)/shard_map/broadcast_in_dim | solution.py:300
  81.2 4.3 %all-to-all-start.1 = ((bf16[128,32,128]{2,1,0:T(8,128)(2,1)}), bf16[128,32,128]{2,1,0:T(8,128)(2,1)S(1)}, u32[]{:S(2)}, u32[]{:S(2)}) async-start(bf16[128,32,128]{2,1,0:T(8,128)(2,1)} %broadcast_in_dim.39), calls=%async_computation.1 | async-start | bytes 2097152 | tf_op jit(solution)/shard_map/all_to_all | solution.py:299
  85.7 4.4 %inputs.1 = f32[64,16,256]{2,1,0:T(8,128)S(1)} custom-call(s32[1]{0:T(128)} %bitcast.1.count, s32[12]{0:T(128)S(1)} %get-tuple-element.11.starts, f32[12]{0:T(128)S(1)} %get-tuple-element.13.alphas, bf16[12,512,256]{2,1,0:T(8,128)(2,1)} %get-tuple-element.8.dpre, bf16[1536,256]{1,0:T(8,128)(2,1)S(1)} %pad_dynamic-update-slice_fusion.w_back), custom_call_target="tpu_custom_call" | custom-call | tf_op jit(solution)/shard_map/inputs/pallas_call | solution.py:221
  90.1 1.6 %collective-permute-start.1 = (bf16[32,16,256]{2,1,0:T(8,128)(2,1)S(1)}, bf16[32,16,256]{2,1,0:T(8,128)(2,1)S(1)}, u32[]{:S(2)}, u32[]{:S(2)}) collective-permute-start(bf16[32,16,256]{2,1,0:T(8,128)(2,1)S(1)} %slice.144), channel_id=1, source_target_pairs={{7,0},{0,1},{1,2},{2,3},{3,4},{4,5},{5,6},{6,7},{15,8},{8,9},{9,10... | collective-permute-start | bytes 786440 | tf_op jit(solution)/shard_map/ppermute | solution.py:29
  91.8 7.7 %collective-permute-done.1 = bf16[32,16,256]{2,1,0:T(8,128)(2,1)S(1)} collective-permute-done((bf16[32,16,256]{2,1,0:T(8,128)(2,1)S(1)}, bf16[32,16,256]{2,1,0:T(8,128)(2,1)S(1)}, u32[]{:S(2)}, u32[]{:S(2)}) %collective-permute-start.1) | collective-permute-done | bytes 262176 | tf_op jit(solution)/shard_map/ppermute | solution.py:29
  99.5 0.3 reshape.182
  99.8 1.1 copy.65
  100.9 4.1 %all-to-all-done.1 = bf16[128,32,128]{2,1,0:T(8,128)(2,1)S(1)} async-done(((bf16[128,32,128]{2,1,0:T(8,128)(2,1)}), bf16[128,32,128]{2,1,0:T(8,128)(2,1)S(1)}, u32[]{:S(2)}, u32[]{:S(2)}) %all-to-all-start.1) | async-done | bytes 1048608 | tf_op jit(solution)/shard_map/all_to_all | solution.py:299
  105.1 0.2 copy.67
  105.3 0.8 copy.83
  106.1 0.3 copy.66
  106.4 0.8 copy.84
  107.3 0.9 bitcast_convert_fusion
  108.1 0.6 bitcast_convert_fusion.1
  108.8 0.6 convert_reduce_fusion.1
  (71 shorter events, 2.4 us)
Async XLA Ops:
  0.6 4.3 %copy-start = (bf16[1152,128]{1,0:T(8,128)(2,1)S(1)}, bf16[1152,128]{1,0:T(8,128)(2,1)}, u32[]{:S(2)}) copy-start(bf16[1152,128]{1,0:T(8,128)(2,1)} %param.12) | copy-start | bytes 884740
  2.0 4.7 %copy-start.5 = (s32[1,32]{1,0:T(1,128)S(1)}, s32[1,32]{1,0:T(1,128)}, u32[]{:S(2)}) copy-start(s32[1,32]{1,0:T(1,128)} %param.10) | copy-start | bytes 388
  2.0 4.9 %copy-start.1 = (bf16[512,256]{1,0:T(8,128)(2,1)S(1)}, bf16[512,256]{1,0:T(8,128)(2,1)}, u32[]{:S(2)}) copy-start(bf16[512,256]{1,0:T(8,128)(2,1)} %param.13) | copy-start | bytes 786436
  3.4 4.0 %copy-start.2 = (bf16[256,512]{1,0:T(8,128)(2,1)S(1)}, bf16[256,512]{1,0:T(8,128)(2,1)}, u32[]{:S(2)}) copy-start(bf16[256,512]{1,0:T(8,128)(2,1)} %param.14) | copy-start | bytes 786436
  3.5 9.5 %collective-permute-start = (bf16[2,32,16,256]{3,2,1,0:T(8,128)(2,1)S(1)}, bf16[2,32,16,256]{3,2,1,0:T(8,128)(2,1)S(1)}, u32[]{:S(2)}, u32[]{:S(2)}) collective-permute-start(bf16[2,32,16,256]{3,2,1,0:T(8,128)(2,1)S(1)} %constant_dynamic-update-slice_fusion), channel_id=1, source_target_pairs={{1,0},{2,1},{3,2},{4,3},{5,4},{6,5},{7,6},{0,7},{9,8},{10,9},{11,1... | collective-permute-start | bytes 1572872 | tf_op jit(solution)/shard_map/ppermute | solution.py:29
  5.4 2.4 %copy-start.3 = (bf16[128,128]{1,0:T(8,128)(2,1)S(1)}, bf16[128,128]{1,0:T(8,128)(2,1)}, u32[]{:S(2)}) copy-start(bf16[128,128]{1,0:T(8,128)(2,1)} %param.15) | copy-start | bytes 98308
  5.4 2.5 %copy-start.4 = (s32[1,32]{1,0:T(1,128)S(1)}, s32[1,32]{1,0:T(1,128)}, u32[]{:S(2)}) copy-start(s32[1,32]{1,0:T(1,128)} %param.11) | copy-start | bytes 388
  24.7 55.1 %all-to-all-start = ((bf16[128,32,128]{2,1,0:T(8,128)(2,1)}), bf16[128,32,128]{2,1,0:T(8,128)(2,1)S(1)}, u32[]{:S(2)}, u32[]{:S(2)}) async-start(bf16[128,32,128]{2,1,0:T(8,128)(2,1)} %bitcast.109), calls=%async_computation | async-start | bytes 2097152 | tf_op jit(solution)/shard_map/all_to_all | solution.py:286
  81.2 23.8 %all-to-all-start.1 = ((bf16[128,32,128]{2,1,0:T(8,128)(2,1)}), bf16[128,32,128]{2,1,0:T(8,128)(2,1)S(1)}, u32[]{:S(2)}, u32[]{:S(2)}) async-start(bf16[128,32,128]{2,1,0:T(8,128)(2,1)} %broadcast_in_dim.39), calls=%async_computation.1 | async-start | bytes 2097152 | tf_op jit(solution)/shard_map/all_to_all | solution.py:299
  90.1 9.3 %collective-permute-start.1 = (bf16[32,16,256]{2,1,0:T(8,128)(2,1)S(1)}, bf16[32,16,256]{2,1,0:T(8,128)(2,1)S(1)}, u32[]{:S(2)}, u32[]{:S(2)}) collective-permute-start(bf16[32,16,256]{2,1,0:T(8,128)(2,1)S(1)} %slice.144), channel_id=1, source_target_pairs={{7,0},{0,1},{1,2},{2,3},{3,4},{4,5},{5,6},{6,7},{15,8},{8,9},{9,10... | collective-permute-start | bytes 786440 | tf_op jit(solution)/shard_map/ppermute | solution.py:29

commit v2 on v1

--- a/solution.py
+++ b/solution.py
@@ -14,7 +14,8 @@
 C = 128
 CELLS = SIDE * HALF
 CHUNK = 32
-NDEV = 128
+NCHIP = 64
+BLOCKS = 16
 
 sigma_low = 0.02
 sigma_high = 20.0
@@ -23,9 +24,13 @@
 f32 = jnp.float32
 
 
+LON = ("x", "core")
+CHIPS = ("lat", "x")
+
+
 def shifted(block, axis, distance):
-    devices = range(lax.axis_size(axis))
-    route = [((i - distance) % len(devices), i) for i in devices]
+    size = lax.axis_size(axis)
+    route = [((i - distance) % size, i) for i in range(size)]
     return lax.ppermute(block, axis, route)
 
 
@@ -80,7 +85,7 @@
 
 
 def patch_kernel(
-    count, starts, alphas, betas,
+    count, parity, starts, alphas, betas,
     feat, noise, w_in, w_dn, w_dn_t, w_u, w_u_t, w_o, w_o_t,
     dpre_out, grads_out,
     slots, first, slope, g_conv, g_down, g_up, g_out, loss,
@@ -139,33 +144,25 @@
 
     lax.fori_loop(0, count[0], one_patch, 0)
 
+    def put(index, block):
+        half = index // BLOCKS
+        grads_out[half ^ parity[0], pl.ds(index % BLOCKS * C, C)] = block.astype(bf16)
+
     for i in range(3):
         for j in range(3):
             block = g_conv[0:C, pl.ds((4 * j + i) * C, C)] + g_conv[C:, pl.ds((4 * j + i + 1) * C, C)]
-            grads_out[pl.ds((3 * i + j) * C, C)] = block.T.astype(bf16)
-    base = 9 * C
+            put(3 * i + j, block.T)
     for a in range(2):
         for b in range(2):
             for h in range(2):
-                block = g_down[h * C : h * C + C, (2 * b + a) * C : (2 * b + a + 1) * C]
-                grads_out[pl.ds(base + ((2 * a + b) * 2 + h) * C, C)] = block.T.astype(bf16)
-    base = 17 * C
-    for a in range(2):
-        for b in range(2):
-            for h in range(2):
-                block = g_up[h * C : h * C + C, (2 * b + a) * C : (2 * b + a + 1) * C]
-                grads_out[pl.ds(base + ((2 * a + b) * 2 + h) * C, C)] = block.astype(bf16)
-    base = 25 * C
-    grads_out[pl.ds(base, C)] = (g_out[0:C, 0:C] + g_out[C:, C:]).astype(bf16)
-    base = 26 * C
-    part = jnp.sum(loss[:, 0:C] + loss[:, C:], axis=0, keepdims=True)
-    high = part.astype(bf16)
-    low = (part - high.astype(f32)).astype(bf16)
-    row = lax.broadcasted_iota(jnp.int32, (C, C), 0)
-    grads_out[pl.ds(base, C)] = jnp.where(
-        row == 0, high.astype(f32), jnp.where(row == 1, low.astype(f32), 0.0)
-    ).astype(bf16)
-    grads_out[pl.ds(27 * C, 5 * C)] = jnp.zeros((5 * C, C), bf16)
+                lanes = pl.ds((2 * b + a) * C, C)
+                put(9 + (2 * a + b) * 2 + h, g_down[h * C : h * C + C, lanes].T)
+                put(17 + (2 * a + b) * 2 + h, g_up[h * C : h * C + C, lanes])
+    put(25, g_out[0:C, 0:C] + g_out[C:, C:])
+    part = loss[:, 0:C] + loss[:, C:]
+    put(26, jnp.concatenate([part, jnp.zeros((C - 8, C), f32)], axis=0))
+    for index in range(27, 2 * BLOCKS):
+        put(index, jnp.zeros((C, C), f32))
 
 
 SLOPE = (HALF, 2, HALF, 2 * C)
@@ -193,14 +190,14 @@
     return pl.BlockSpec(memory_space=pltpu.VMEM)
 
 
-def run_patches(count, starts, alphas, betas, feat, noise, weights):
+def run_patches(count, parity, starts, alphas, betas, feat, noise, weights):
     return pl.pallas_call(
         patch_kernel,
         out_shape=(
             jax.ShapeDtypeStruct((PMAX, CELLS, 2 * C), bf16),
-            jax.ShapeDtypeStruct((NDEV * CHUNK, C), bf16),
+            jax.ShapeDtypeStruct((2, BLOCKS * C, C), bf16),
         ),
-        in_specs=[smem()] * 4 + [vmem()] * 9,
+        in_specs=[smem()] * 5 + [vmem()] * 9,
         out_specs=(vmem(), vmem()),
         scratch_shapes=[
             pltpu.VMEM((SIDE + 2, HALF, 4 * C), bf16),
@@ -214,7 +211,7 @@
         ],
         compiler_params=pltpu.CompilerParams(vmem_limit_bytes=50 << 20),
         name="patches",
-    )(count, starts, alphas, betas, feat, noise, *weights)
+    )(count, parity, starts, alphas, betas, feat, noise, *weights)
 
 
 def run_inputs(count, starts, alphas, dpre, w_back):
@@ -229,6 +226,40 @@
     )(count, starts, alphas, dpre, w_back)
 
 
+def run_finish(parity, half, other, cells):
+    def finish_kernel(parity, mine, theirs, conv, down, up, out, loss):
+        def write(low, high):
+            def get(index):
+                ref = (low, high)[index // BLOCKS]
+                return ref[pl.ds(index % BLOCKS * C, C)].astype(f32)
+
+            for index in range(9):
+                conv[pl.ds(index * C, C)] = get(index)
+            for q in range(4):
+                for h in range(2):
+                    down[pl.ds(q * C, C), pl.ds(h * C, C)] = get(9 + 2 * q + h)
+                    up[pl.ds(h * C, C), pl.ds(q * C, C)] = get(17 + 2 * q + h)
+            out[...] = get(25)
+            loss[0] = jnp.sum(get(26)[0:8]) * (0.5 / (C * cells))
+
+        pl.when(parity[0] == 0)(lambda: write(mine, theirs))
+        pl.when(parity[0] == 1)(lambda: write(theirs, mine))
+
+    return pl.pallas_call(
+        finish_kernel,
+        out_shape=(
+            jax.ShapeDtypeStruct((9 * C, C), f32),
+            jax.ShapeDtypeStruct((4 * C, 2 * C), f32),
+            jax.ShapeDtypeStruct((2 * C, 4 * C), f32),
+            jax.ShapeDtypeStruct((C, C), f32),
+            jax.ShapeDtypeStruct((1,), f32),
+        ),
+        in_specs=[smem(), vmem(), vmem()],
+        out_specs=(vmem(), vmem(), vmem(), vmem(), smem()),
+        name="finish",
+    )(parity, half, other)
+
+
 def layout_weights(w_conv, w_down, w_up, w_out):
     zero = jnp.zeros((C, C), bf16)
     conv = w_conv.reshape(3, 3, C, C)
@@ -262,12 +293,12 @@
 
 def per_device(encoder_features, noise, patch_cols, timesteps, w_conv, w_down, w_up, w_out):
     block_cols = encoder_features.shape[1]
-    lon_index = lax.axis_index("lon")
+    lon_index = lax.axis_index(LON)
     starts_all = patch_cols[0]
     band_patches = starts_all.shape[0]
 
     both = jnp.stack([pack_rows(encoder_features), pack_rows(noise)])
-    nxt = shifted(both, "lon", -1)
+    nxt = shifted(both, LON, -1)
     window = jnp.concatenate([both, nxt], axis=1)
 
     mine = (starts_all // block_cols) == lon_index
@@ -276,59 +307,39 @@
     starts = jnp.sum(jnp.where(pick, starts_all[None, :] - lon_index * block_cols, 0), axis=1)
     levels = jnp.sum(jnp.where(pick, timesteps[0][None, :], 0), axis=1)
     count = jnp.sum(mine.astype(jnp.int32)).reshape(1)
+    parity = lax.axis_index("core").reshape(1)
     sigma = sigma_of(levels)
     alphas = 1.0 / jnp.sqrt(1.0 + sigma * sigma)
     betas = alphas * sigma
 
     weights, w_back = layout_weights(w_conv, w_down, w_up, w_out)
-    dpre, grads = run_patches(count, starts, alphas, betas, window[0], window[1], weights)
-
-    chunks = lax.all_to_all(grads.reshape(NDEV, CHUNK, C), ("lat", "lon"), 0, 0, tiled=True)
+    dpre, grads = run_patches(count, parity, starts, alphas, betas, window[0], window[1], weights)
+
+    theirs = shifted(grads[1], "core", 1)
+    chip = (grads[0].astype(f32) + theirs.astype(f32)).astype(bf16)
+    chunks = lax.all_to_all(chip.reshape(NCHIP, CHUNK, C), CHIPS, 0, 0, tiled=True)
     grad_win = run_inputs(count, starts, alphas, dpre, w_back)
-    returned = shifted(grad_win[block_cols:].astype(bf16), "lon", 1)
+    returned = shifted(grad_win[block_cols:].astype(bf16), LON, 1)
     feature_grad = unpack_rows(grad_win[:block_cols] + returned.astype(f32))
 
-    mean = jnp.sum(chunks.astype(f32), axis=0)
-    high = mean.astype(bf16)
-    total = mean[0:2].sum(axis=0)
-    total_high = total.astype(bf16)
-    total_low = (total - total_high.astype(f32)).astype(bf16)
-    device = lax.axis_index("lat") * lax.axis_size("lon") + lon_index
-    fixed = jnp.concatenate([total_high[None], total_low[None], high[2:]], axis=0)
-    high = jnp.where(device == 26 * C // CHUNK, fixed, high)
-    sums = lax.all_to_all(
-        jnp.broadcast_to(high[None], (NDEV, CHUNK, C)), ("lat", "lon"), 0, 0, tiled=True
-    ).reshape(NDEV * CHUNK, C)
-
-    grad_conv = sums[: 9 * C].astype(f32)
-    grad_down = (
-        sums[9 * C : 17 * C].astype(f32).reshape(4, 2, C, C).transpose(0, 2, 1, 3).reshape(4 * C, 2 * C)
-    )
-    grad_up = (
-        sums[17 * C : 25 * C].astype(f32).reshape(4, 2, C, C).transpose(1, 2, 0, 3).reshape(2 * C, 4 * C)
-    )
-    grad_out = sums[25 * C : 26 * C].astype(f32)
-    objective = jnp.sum(sums[26 * C : 26 * C + 2].astype(f32)) / (2.0 * C)
-    side = encoder_features.shape[0]
-    loss_value = objective / (lax.axis_size("lat") * band_patches * side * side)
-    return (feature_grad, grad_conv, grad_down, grad_up, grad_out, loss_value)
+    total = jnp.sum(chunks.astype(f32), axis=0).astype(bf16)
+    half = lax.all_to_all(
+        jnp.broadcast_to(total[None], (NCHIP, CHUNK, C)), CHIPS, 0, 0, tiled=True
+    ).reshape(BLOCKS * C, C)
+    other = shifted(half, "core", 1)
+    cells = lax.axis_size("lat") * band_patches * encoder_features.shape[0] ** 2
+    grad_conv, grad_down, grad_up, grad_out, loss = run_finish(parity, half, other, cells)
+    return (feature_grad, grad_conv, grad_down, grad_up, grad_out, loss.reshape(()))
 
 
 def solution(mesh):
-    placed = (
-        P("lat", "lon", None),
-        P("lat", "lon", None),
-        P("lat", None),
-        P("lat", None),
-        P(),
-        P(),
-        P(),
-        P(),
-    )
+    lats, lons = mesh.devices.shape
+    chips = jax.sharding.Mesh(mesh.devices.reshape(lats, lons // 2, 2), ("lat", "x", "core"))
+    field = P("lat", LON, None)
     return jax.shard_map(
         per_device,
-        mesh=mesh,
-        in_specs=placed,
-        out_specs=(P("lat", "lon", None), P(), P(), P(), P(), P()),
+        mesh=chips,
+        in_specs=(field, field, P("lat", None), P("lat", None), P(), P(), P(), P()),
+        out_specs=(field, P(), P(), P(), P(), P()),
         check_vma=False,
     )

time: 112 us -> 115 us (1.027)
  the two profiles are of different devices: /device:TPU:1 before, /device:TPU:0 now
where the time goes in v2:
time: 115 us; the launch traced here: 117 us
  Pallas kernels  49.1 us (43%)
  waiting for transfers between devices  37.5 us (33%)
  starting transfers between devices  16.4 us (14%)
  local copies, waits for them, and re-layouts  9.43 us (8%)
  other arithmetic  3.42 us (3%)
    pallas_call x1, Pallas kernels, run_patches(): pl.pallas_call(patch_kernel, out_shape=(jax.ShapeDtypeStruct((PMAX, CELLS...  36.7 us
    all_to_all x1, waiting for transfers between devices, per_device(): lax.all_to_all(chip.reshape(NCHIP, CHUNK, C), CHIPS, 0, 0, tiled=True)  13.6 us
    all_to_all x1, waiting for transfers between devices, per_device(): lax.all_to_all(jnp.broadcast_to(total[None], (NCHIP, CHUNK, C)), CHIPS, 0...  12.2 us
    ppermute x4, waiting for transfers between devices, shifted(): return lax.ppermute(block, axis, route)  11.7 us
    pallas_call x1, Pallas kernels, run_inputs(): pl.pallas_call(input_kernel, out_shape=jax.ShapeDtypeStruct((2 * SIDE, HA...  9.73 us
    all_to_all x1, starting transfers between devices, per_device(): lax.all_to_all(chip.reshape(NCHIP, CHUNK, C), CHIPS, 0, 0, tiled=True)  9.23 us
    all_to_all x1, starting transfers between devices, per_device(): lax.all_to_all(jnp.broadcast_to(total[None], (NCHIP, CHUNK, C)), CHIPS, 0...  4.73 us
    pallas_call x1, Pallas kernels, run_finish(): pl.pallas_call(finish_kernel, out_shape=(jax.ShapeDtypeStruct((9 * C, C),...  2.63 us
  transfers between devices with their start and end apart: 6, of which 5 were waited for; matrix products, arithmetic and copies ran while one was open for 4% of the time, Pallas kernels for 8%

profile of v2, /device:TPU:0, one launch (start us, length us, event | category | flops | bytes accessed | tf_op | source)
XLA Modules:
  0.0 117.0 jit_solution(11555131343048696269)
XLA Ops:
  0.6 1.2 %copy.74 = bf16[16,2,32,128]{3,1,0,2:T(2,128)(2,1)S(1)} copy(bf16[16,2,32,128]{3,2,1,0:T(8,128)(2,1)} %bitcast.127) | data formatting | bytes 524288 | tf_op jit(solution)/shard_map/reshape | solution.py:53
  1.8 0.2 stack_reshape.6
  2.1 1.2 %copy.73 = bf16[16,2,32,128]{3,1,0,2:T(2,128)(2,1)S(1)} copy(bf16[16,2,32,128]{3,2,1,0:T(8,128)(2,1)} %bitcast.128) | data formatting | bytes 524288 | tf_op jit(solution)/shard_map/reshape | solution.py:53
  3.3 0.2 stack_reshape.7
  3.5 2.3 %collective-permute-start = (bf16[2,32,16,256]{3,2,1,0:T(8,128)(2,1)S(1)}, bf16[2,32,16,256]{3,2,1,0:T(8,128)(2,1)S(1)}, u32[]{:S(2)}, u32[]{:S(2)}) collective-permute-start(bf16[2,32,16,256]{3,2,1,0:T(8,128)(2,1)S(1)} %constant_dynamic-update-slice_fusion), channel_id=1, source_target_pairs={{1,0},{2,1},{3,2},{4,3},{5,4},{6,5},{7,6},{0,7},{9,8},{10,9},{11,1... | collective-permute-start | bytes 1572872 | tf_op jit(solution)/shard_map/ppermute | solution.py:34
  6.1 0.1 copy.64
  6.4 0.1 copy.66
  6.5 0.1 copy.67
  6.9 0.1 copy.69
  7.0 0.1 copy.70
  7.2 0.3 copy.58.w_in
  7.8 0.2 copy.55
  8.1 0.1 copy.59.w_dn
  8.3 0.2 copy.56
  8.5 0.1 copy.60.w_u
  8.9 0.6 fusion.12
  9.6 2.9 %collective-permute-done = bf16[2,32,16,256]{3,2,1,0:T(8,128)(2,1)S(1)} collective-permute-done((bf16[2,32,16,256]{3,2,1,0:T(8,128)(2,1)S(1)}, bf16[2,32,16,256]{3,2,1,0:T(8,128)(2,1)S(1)}, u32[]{:S(2)}, u32[]{:S(2)}) %collective-permute-start) | collective-permute-done | bytes 524320 | tf_op jit(solution)/shard_map/ppermute | solution.py:34
  12.6 36.7 %patches.1 = (bf16[12,512,256]{2,1,0:T(8,128)(2,1)}, bf16[2,2048,128]{2,1,0:T(8,128)(2,1)}) custom-call(s32[1]{0:T(128)} %bitcast.1.count, s32[1]{0:T(128)} %bitcast.6.parity, s32[12]{0:T(128)S(1)} %get-tuple-element.21.starts, f32[12]{0:T(128)S(1)} %get-tuple-element.23.alphas, f32[12]{0:T(128)S(1)} %get-tuple-element.22.betas, ...), custom_call_target="tpu_custom_call" | custom-call | tf_op jit(solution)/shard_map/patches/pallas_call | solution.py:194
  49.3 1.1 slice_bitcast_fusion
  50.5 1.9 %collective-permute-done.2 = bf16[2048,128]{1,0:T(8,128)(2,1)S(1)} collective-permute-done((bf16[2048,128]{1,0:T(8,128)(2,1)S(1)}, bf16[2048,128]{1,0:T(8,128)(2,1)S(1)}, u32[]{:S(2)}, u32[]{:S(2)}) %collective-permute-start.2) | collective-permute-done | bytes 524320 | tf_op jit(solution)/shard_map/ppermute | solution.py:34
  52.3 2.0 %fusion = bf16[2048,128]{1,0:T(8,128)(2,1)} fusion(bf16[2048,128]{1,0:T(8,128)(2,1)S(1)} %collective-permute-done.2, bf16[2,2048,128]{2,1,0:T(8,128)(2,1)} %get-tuple-element.14), kind=kLoop, calls=%fused_computation.3 | loop fusion | flops 1048576 | bytes 1572864 | tf_op jit(solution)/shard_map/convert_element_type | solution.py:319
  54.3 9.2 %all-to-all-start = ((bf16[64,32,128]{2,1,0:T(8,128)(2,1)}), bf16[64,32,128]{2,1,0:T(8,128)(2,1)S(1)}, u32[]{:S(2)}, u32[]{:S(2)}) async-start(bf16[64,32,128]{2,1,0:T(8,128)(2,1)} %bitcast.53), calls=%async_computation | async-start | bytes 1048576 | tf_op jit(solution)/shard_map/all_to_all | solution.py:320
  63.6 13.6 %all-to-all-done = bf16[64,32,128]{2,1,0:T(8,128)(2,1)S(1)} async-done(((bf16[64,32,128]{2,1,0:T(8,128)(2,1)}), bf16[64,32,128]{2,1,0:T(8,128)(2,1)S(1)}, u32[]{:S(2)}, u32[]{:S(2)}) %all-to-all-start) | async-done | bytes 524320 | tf_op jit(solution)/shard_map/all_to_all | solution.py:320
  77.3 0.9 broadcast_in_dim.37
  78.2 4.7 %all-to-all-start.1 = ((bf16[64,32,128]{2,1,0:T(8,128)(2,1)}), bf16[64,32,128]{2,1,0:T(8,128)(2,1)S(1)}, u32[]{:S(2)}, u32[]{:S(2)}) async-start(bf16[64,32,128]{2,1,0:T(8,128)(2,1)} %broadcast_in_dim.37), calls=%async_computation.1 | async-start | bytes 1048576 | tf_op jit(solution)/shard_map/all_to_all | solution.py:326
  83.0 12.2 %all-to-all-done.1 = bf16[64,32,128]{2,1,0:T(8,128)(2,1)S(1)} async-done(((bf16[64,32,128]{2,1,0:T(8,128)(2,1)}), bf16[64,32,128]{2,1,0:T(8,128)(2,1)S(1)}, u32[]{:S(2)}, u32[]{:S(2)}) %all-to-all-start.1) | async-done | bytes 524320 | tf_op jit(solution)/shard_map/all_to_all | solution.py:326
  95.3 9.7 %inputs.1 = f32[64,16,256]{2,1,0:T(8,128)S(1)} custom-call(s32[1]{0:T(128)} %bitcast.1.count, s32[12]{0:T(128)S(1)} %get-tuple-element.21.starts, f32[12]{0:T(128)S(1)} %get-tuple-element.23.alphas, bf16[12,512,256]{2,1,0:T(8,128)(2,1)} %get-tuple-element.13.dpre, bf16[1536,256]{1,0:T(8,128)(2,1)S(1)} %pad_dynamic-update-slice_fusion.w_back), custom_call_target="tpu_custom_call" | custom-call | tf_op jit(solution)/shard_map/inputs/pallas_call | solution.py:218
  105.1 7.0 %collective-permute-done.1 = bf16[32,16,256]{2,1,0:T(8,128)(2,1)S(1)} collective-permute-done((bf16[32,16,256]{2,1,0:T(8,128)(2,1)S(1)}, bf16[32,16,256]{2,1,0:T(8,128)(2,1)S(1)}, u32[]{:S(2)}, u32[]{:S(2)}) %collective-permute-start.1) | collective-permute-done | bytes 262176 | tf_op jit(solution)/shard_map/ppermute | solution.py:34
  112.2 0.3 reshape.119
  112.4 1.1 copy.61
  113.5 0.8 copy-done.1
  114.3 2.6 %finish.1 = (f32[1152,128]{1,0:T(8,128)}, f32[512,256]{1,0:T(8,128)}, f32[256,512]{1,0:T(8,128)}, f32[128,128]{1,0:T(8,128)}, f32[1]{0:T(128)}) custom-call(s32[1]{0:T(128)} %bitcast.6.parity, bf16[2048,128]{1,0:T(8,128)(2,1)} %bitcast.84, bf16[2048,128]{1,0:T(8,128)(2,1)} %copy-done.1), custom_call_target="tpu_custom_call" | custom-call | tf_op jit(solution)/shard_map/finish/pallas_call | solution.py:248
  (66 shorter events, 2.0 us)
Async XLA Ops:
  0.6 5.1 %copy-start.2 = (bf16[1152,128]{1,0:T(8,128)(2,1)S(1)}, bf16[1152,128]{1,0:T(8,128)(2,1)}, u32[]{:S(2)}) copy-start(bf16[1152,128]{1,0:T(8,128)(2,1)} %param.12) | copy-start | bytes 884740
  2.0 5.5 %copy-start.7 = (s32[1,32]{1,0:T(1,128)S(1)}, s32[1,32]{1,0:T(1,128)}, u32[]{:S(2)}) copy-start(s32[1,32]{1,0:T(1,128)} %param.10) | copy-start | bytes 388
  2.0 5.8 %copy-start.3 = (bf16[512,256]{1,0:T(8,128)(2,1)S(1)}, bf16[512,256]{1,0:T(8,128)(2,1)}, u32[]{:S(2)}) copy-start(bf16[512,256]{1,0:T(8,128)(2,1)} %param.13) | copy-start | bytes 786436
  3.4 4.8 %copy-start.4 = (bf16[256,512]{1,0:T(8,128)(2,1)S(1)}, bf16[256,512]{1,0:T(8,128)(2,1)}, u32[]{:S(2)}) copy-start(bf16[256,512]{1,0:T(8,128)(2,1)} %param.14) | copy-start | bytes 786436
  3.5 9.0 %collective-permute-start = (bf16[2,32,16,256]{3,2,1,0:T(8,128)(2,1)S(1)}, bf16[2,32,16,256]{3,2,1,0:T(8,128)(2,1)S(1)}, u32[]{:S(2)}, u32[]{:S(2)}) collective-permute-start(bf16[2,32,16,256]{3,2,1,0:T(8,128)(2,1)S(1)} %constant_dynamic-update-slice_fusion), channel_id=1, source_target_pairs={{1,0},{2,1},{3,2},{4,3},{5,4},{6,5},{7,6},{0,7},{9,8},{10,9},{11,1... | collective-permute-start | bytes 1572872 | tf_op jit(solution)/shard_map/ppermute | solution.py:34
  6.2 2.4 %copy-start.5 = (bf16[128,128]{1,0:T(8,128)(2,1)S(1)}, bf16[128,128]{1,0:T(8,128)(2,1)}, u32[]{:S(2)}) copy-start(bf16[128,128]{1,0:T(8,128)(2,1)} %param.15) | copy-start | bytes 98308
  6.3 2.5 %copy-start.6 = (s32[1,32]{1,0:T(1,128)S(1)}, s32[1,32]{1,0:T(1,128)}, u32[]{:S(2)}) copy-start(s32[1,32]{1,0:T(1,128)} %param.11) | copy-start | bytes 388
  50.4 2.0 %collective-permute-start.2 = (bf16[2048,128]{1,0:T(8,128)(2,1)S(1)}, bf16[2048,128]{1,0:T(8,128)(2,1)S(1)}, u32[]{:S(2)}, u32[]{:S(2)}) collective-permute-start(bf16[2048,128]{1,0:T(8,128)(2,1)S(1)} %slice_bitcast_fusion), channel_id=1, source_target_pairs={{1,0},{0,1},{3,2},{2,3},{5,4},{4,5},{7,6},{6,7},{9,8},{8,9},{11,10... | collective-permute-start | bytes 1572872 | tf_op jit(solution)/shard_map/ppermute | solution.py:34
  54.3 22.9 %all-to-all-start = ((bf16[64,32,128]{2,1,0:T(8,128)(2,1)}), bf16[64,32,128]{2,1,0:T(8,128)(2,1)S(1)}, u32[]{:S(2)}, u32[]{:S(2)}) async-start(bf16[64,32,128]{2,1,0:T(8,128)(2,1)} %bitcast.53), calls=%async_computation | async-start | bytes 1048576 | tf_op jit(solution)/shard_map/all_to_all | solution.py:320
  78.2 17.1 %all-to-all-start.1 = ((bf16[64,32,128]{2,1,0:T(8,128)(2,1)}), bf16[64,32,128]{2,1,0:T(8,128)(2,1)S(1)}, u32[]{:S(2)}, u32[]{:S(2)}) async-start(bf16[64,32,128]{2,1,0:T(8,128)(2,1)} %broadcast_in_dim.37), calls=%async_computation.1 | async-start | bytes 1048576 | tf_op jit(solution)/shard_map/all_to_all | solution.py:326
  95.3 16.9 %copy-start = (bf16[64,32,128]{2,1,0:T(8,128)(2,1)}, bf16[64,32,128]{2,1,0:T(8,128)(2,1)S(1)}, u32[]{:S(2)}) copy-start(bf16[64,32,128]{2,1,0:T(8,128)(2,1)S(1)} %all-to-all-done.1) | copy-start | bytes 1572868
  95.3 18.3 %collective-permute-start.3 = (bf16[2048,128]{1,0:T(8,128)(2,1)S(1)}, bf16[2048,128]{1,0:T(8,128)(2,1)S(1)}, u32[]{:S(2)}, u32[]{:S(2)}) collective-permute-start(bf16[2048,128]{1,0:T(8,128)(2,1)S(1)} %bitcast.83), channel_id=1, source_target_pairs={{1,0},{0,1},{3,2},{2,3},{5,4},{4,5},{7,6},{6,7},{9,8},{8,9},{11,10... | collective-permute-start | bytes 1572872 | tf_op jit(solution)/shard_map/ppermute | solution.py:34
  105.0 7.0 %collective-permute-start.1 = (bf16[32,16,256]{2,1,0:T(8,128)(2,1)S(1)}, bf16[32,16,256]{2,1,0:T(8,128)(2,1)S(1)}, u32[]{:S(2)}, u32[]{:S(2)}) collective-permute-start(bf16[32,16,256]{2,1,0:T(8,128)(2,1)S(1)} %slice.113), channel_id=1, source_target_pairs={{7,0},{0,1},{1,2},{2,3},{3,4},{4,5},{5,6},{6,7},{15,8},{8,9},{9,10... | collective-permute-start | bytes 786440 | tf_op jit(solution)/shard_map/ppermute | solution.py:34
  113.5 0.8 copy-start.1

commit v3 on v2

--- a/solution.py
+++ b/solution.py
@@ -317,8 +317,10 @@
 
     theirs = shifted(grads[1], "core", 1)
     chip = (grads[0].astype(f32) + theirs.astype(f32)).astype(bf16)
+    chip, dpre = lax.optimization_barrier((chip, dpre))
     chunks = lax.all_to_all(chip.reshape(NCHIP, CHUNK, C), CHIPS, 0, 0, tiled=True)
     grad_win = run_inputs(count, starts, alphas, dpre, w_back)
+    chunks, grad_win = lax.optimization_barrier((chunks, grad_win))
     returned = shifted(grad_win[block_cols:].astype(bf16), LON, 1)
     feature_grad = unpack_rows(grad_win[:block_cols] + returned.astype(f32))
 
@@ -326,6 +328,7 @@
     half = lax.all_to_all(
         jnp.broadcast_to(total[None], (NCHIP, CHUNK, C)), CHIPS, 0, 0, tiled=True
     ).reshape(BLOCKS * C, C)
+    half, feature_grad = lax.optimization_barrier((half, feature_grad))
     other = shifted(half, "core", 1)
     cells = lax.axis_size("lat") * band_patches * encoder_features.shape[0] ** 2
     grad_conv, grad_down, grad_up, grad_out, loss = run_finish(parity, half, other, cells)

time: 115 us -> 109 us (0.948)
  the two profiles are of different devices: /device:TPU:0 before, /device:TPU:1 now
where the time goes in v3:
time: 109 us; the launch traced here: 108 us
  Pallas kernels  49 us (45%)
  waiting for transfers between devices  22.5 us (21%)
  starting transfers between devices  22 us (20%)
  local copies, waits for them, and re-layouts  9.44 us (9%)
  other arithmetic  4.44 us (4%)
  between operations  1.13 us (1%)
    pallas_call x1, Pallas kernels, run_patches(): pl.pallas_call(patch_kernel, out_shape=(jax.ShapeDtypeStruct((PMAX, CELLS...  36.7 us
    all_to_all x1, starting transfers between devices, per_device(): lax.all_to_all(chip.reshape(NCHIP, CHUNK, C), CHIPS, 0, 0, tiled=True)  12.1 us
    all_to_all x1, waiting for transfers between devices, per_device(): lax.all_to_all(jnp.broadcast_to(total[None], (NCHIP, CHUNK, C)), CHIPS, 0...  11.8 us
    pallas_call x1, Pallas kernels, run_inputs(): pl.pallas_call(input_kernel, out_shape=jax.ShapeDtypeStruct((2 * SIDE, HA...  9.66 us
    ppermute x4, waiting for transfers between devices, shifted(): return lax.ppermute(block, axis, route)  7.71 us
    all_to_all x1, starting transfers between devices, per_device(): lax.all_to_all(jnp.broadcast_to(total[None], (NCHIP, CHUNK, C)), CHIPS, 0...  6.29 us
    ppermute x4, starting transfers between devices, shifted(): return lax.ppermute(block, axis, route)  3.66 us
    all_to_all x1, waiting for transfers between devices, per_device(): lax.all_to_all(chip.reshape(NCHIP, CHUNK, C), CHIPS, 0, 0, tiled=True)  2.91 us
  transfers between devices with their start and end apart: 6, of which 5 were waited for; matrix products, arithmetic and copies ran while one was open for 6% of the time, Pallas kernels for 9%

profile of v3, /device:TPU:1, one launch (start us, length us, event | category | flops | bytes accessed | tf_op | source)
XLA Modules:
  0.0 108.4 jit_solution(8152800286553315552)
XLA Ops:
  0.7 1.2 %copy.74 = bf16[16,2,32,128]{3,1,0,2:T(2,128)(2,1)S(1)} copy(bf16[16,2,32,128]{3,2,1,0:T(8,128)(2,1)} %bitcast.127) | data formatting | bytes 524288 | tf_op jit(solution)/shard_map/reshape | solution.py:53
  1.9 0.2 stack_reshape.6
  2.1 1.2 %copy.73 = bf16[16,2,32,128]{3,1,0,2:T(2,128)(2,1)S(1)} copy(bf16[16,2,32,128]{3,2,1,0:T(8,128)(2,1)} %bitcast.128) | data formatting | bytes 524288 | tf_op jit(solution)/shard_map/reshape | solution.py:53
  3.3 0.2 stack_reshape.7
  3.5 1.4 %collective-permute-start = (bf16[2,32,16,256]{3,2,1,0:T(8,128)(2,1)S(1)}, bf16[2,32,16,256]{3,2,1,0:T(8,128)(2,1)}, u32[]{:S(2)}, u32[]{:S(2)}) collective-permute-start(bf16[2,32,16,256]{3,2,1,0:T(8,128)(2,1)S(1)} %constant_dynamic-update-slice_fusion), channel_id=1, source_target_pairs={{1,0},{2,1},{3,2},{4,3},{5,4},{6,5},{7,6},{0,7},{9,8},{10,9},{11,1... | collective-permute-start | bytes 1572872 | tf_op jit(solution)/shard_map/ppermute | solution.py:34
  4.9 0.6 fusion.12
  5.9 0.1 copy.64
  6.3 0.1 copy.67
  7.0 0.3 copy.58.w_in
  7.6 0.2 copy.55
  7.9 0.1 copy.59.w_dn
  8.1 0.2 copy.56
  8.3 0.1 copy.60.w_u
  8.8 4.3 %collective-permute-done = bf16[2,32,16,256]{3,2,1,0:T(8,128)(2,1)} collective-permute-done((bf16[2,32,16,256]{3,2,1,0:T(8,128)(2,1)S(1)}, bf16[2,32,16,256]{3,2,1,0:T(8,128)(2,1)}, u32[]{:S(2)}, u32[]{:S(2)}) %collective-permute-start) | collective-permute-done | bytes 524320 | tf_op jit(solution)/shard_map/ppermute | solution.py:34
  13.1 1.1 %fusion.3 = (bf16[64,16,256]{2,1,0:T(8,128)(2,1)S(1)}, bf16[64,16,256]{2,1,0:T(8,128)(2,1)S(1)}) fusion(bf16[2,32,16,256]{3,2,1,0:T(8,128)(2,1)} %collective-permute-done, bf16[2,32,16,256]{3,2,1,0:T(8,128)(2,1)S(1)} %constant_dynamic-update-slice_fusion), kind=kLoop, calls=%fused_computation.8 | loop fusion | flops 524288 | bytes 2097152 | tf_op jit(solution)/shard_map/squeeze | solution.py:316
  14.2 36.7 %patches.1 = (bf16[12,512,256]{2,1,0:T(8,128)(2,1)}, bf16[2,2048,128]{2,1,0:T(8,128)(2,1)}) custom-call(s32[1]{0:T(128)} %bitcast.1.count, s32[1]{0:T(128)} %bitcast.2.parity, s32[12]{0:T(128)S(1)} %get-tuple-element.33.starts, f32[12]{0:T(128)S(1)} %get-tuple-element.35.alphas, f32[12]{0:T(128)S(1)} %get-tuple-element.34.betas, ...), custom_call_target="tpu_custom_call" | custom-call | tf_op jit(solution)/shard_map/patches/pallas_call | solution.py:194
  50.9 1.1 slice_bitcast_fusion
  52.2 1.8 %collective-permute-done.1 = bf16[2048,128]{1,0:T(8,128)(2,1)S(1)} collective-permute-done((bf16[2048,128]{1,0:T(8,128)(2,1)S(1)}, bf16[2048,128]{1,0:T(8,128)(2,1)S(1)}, u32[]{:S(2)}, u32[]{:S(2)}) %collective-permute-start.1) | collective-permute-done | bytes 524320 | tf_op jit(solution)/shard_map/ppermute | solution.py:34
  54.0 2.0 %fusion = bf16[2048,128]{1,0:T(8,128)(2,1)} fusion(bf16[2048,128]{1,0:T(8,128)(2,1)S(1)} %collective-permute-done.1, bf16[2,2048,128]{2,1,0:T(8,128)(2,1)} %get-tuple-element.19), kind=kLoop, calls=%fused_computation.3 | loop fusion | flops 1048576 | bytes 1572864 | tf_op jit(solution)/shard_map/convert_element_type | solution.py:319
  55.9 12.1 %all-to-all-start = ((bf16[64,32,128]{2,1,0:T(8,128)(2,1)}), bf16[64,32,128]{2,1,0:T(8,128)(2,1)S(1)}, u32[]{:S(2)}, u32[]{:S(2)}) async-start(bf16[64,32,128]{2,1,0:T(8,128)(2,1)} %bitcast.33), calls=%async_computation | async-start | bytes 1048576 | tf_op jit(solution)/shard_map/all_to_all | solution.py:321
  68.1 9.7 %inputs.1 = f32[64,16,256]{2,1,0:T(8,128)S(1)} custom-call(s32[1]{0:T(128)} %bitcast.1.count, s32[12]{0:T(128)S(1)} %get-tuple-element.33.starts, f32[12]{0:T(128)S(1)} %get-tuple-element.35.alphas, bf16[12,512,256]{2,1,0:T(8,128)(2,1)} %get-tuple-element.22.dpre, bf16[1536,256]{1,0:T(8,128)(2,1)S(1)} %pad_dynamic-update-slice_fusion.w_back), custom_call_target="tpu_custom_call" | custom-call | tf_op jit(solution)/shard_map/inputs/pallas_call | solution.py:218
  77.8 2.9 %all-to-all-done = bf16[64,32,128]{2,1,0:T(8,128)(2,1)S(1)} async-done(((bf16[64,32,128]{2,1,0:T(8,128)(2,1)}), bf16[64,32,128]{2,1,0:T(8,128)(2,1)S(1)}, u32[]{:S(2)}, u32[]{:S(2)}) %all-to-all-start) | async-done | bytes 524320 | tf_op jit(solution)/shard_map/all_to_all | solution.py:321
  80.7 1.8 %collective-permute-start.2 = (bf16[32,16,256]{2,1,0:T(8,128)(2,1)S(1)}, bf16[32,16,256]{2,1,0:T(8,128)(2,1)S(1)}, u32[]{:S(2)}, u32[]{:S(2)}) collective-permute-start(bf16[32,16,256]{2,1,0:T(8,128)(2,1)S(1)} %slice.112), channel_id=1, source_target_pairs={{7,0},{0,1},{1,2},{2,3},{3,4},{4,5},{5,6},{6,7},{15,8},{8,9},{9,10... | collective-permute-start | bytes 786440 | tf_op jit(solution)/shard_map/ppermute | solution.py:34
  82.6 0.9 broadcast_in_dim.37
  83.5 6.3 %all-to-all-start.1 = ((bf16[64,32,128]{2,1,0:T(8,128)(2,1)}), bf16[64,32,128]{2,1,0:T(8,128)(2,1)S(1)}, u32[]{:S(2)}, u32[]{:S(2)}) async-start(bf16[64,32,128]{2,1,0:T(8,128)(2,1)} %broadcast_in_dim.37), calls=%async_computation.1 | async-start | bytes 1048576 | tf_op jit(solution)/shard_map/all_to_all | solution.py:328
  89.9 0.3 reshape.121
  90.2 1.1 %copy.61 = f32[16,2,32,128]{3,2,1,0:T(8,128)} copy(f32[16,2,32,128]{3,1,0,2:T(2,128)S(1)} %bitcast.85) | data formatting | bytes 1048576 | tf_op jit(solution)/shard_map/transpose | solution.py:60
  91.3 11.8 %all-to-all-done.1 = bf16[64,32,128]{2,1,0:T(8,128)(2,1)S(1)} async-done(((bf16[64,32,128]{2,1,0:T(8,128)(2,1)}), bf16[64,32,128]{2,1,0:T(8,128)(2,1)S(1)}, u32[]{:S(2)}, u32[]{:S(2)}) %all-to-all-start.1) | async-done | bytes 524320 | tf_op jit(solution)/shard_map/all_to_all | solution.py:328
  103.1 0.3 collective-permute-start.3
  103.4 1.6 %collective-permute-done.3.theirs = bf16[2048,128]{1,0:T(8,128)(2,1)S(1)} collective-permute-done((bf16[2048,128]{1,0:T(8,128)(2,1)S(1)}, bf16[2048,128]{1,0:T(8,128)(2,1)S(1)}, u32[]{:S(2)}, u32[]{:S(2)}) %collective-permute-start.3) | collective-permute-done | bytes 524320 | tf_op jit(solution)/shard_map/ppermute | solution.py:34
  105.0 0.8 copy-done.1
  105.8 2.6 %finish.1 = (f32[1152,128]{1,0:T(8,128)}, f32[512,256]{1,0:T(8,128)}, f32[256,512]{1,0:T(8,128)}, f32[128,128]{1,0:T(8,128)}, f32[1]{0:T(128)}) custom-call(s32[1]{0:T(128)} %bitcast.2.parity, bf16[2048,128]{1,0:T(8,128)(2,1)} %bitcast.84, bf16[2048,128]{1,0:T(8,128)(2,1)} %copy-done.1), custom_call_target="tpu_custom_call" | custom-call | tf_op jit(solution)/shard_map/finish/pallas_call | solution.py:248
  (66 shorter events, 2.3 us)
Async XLA Ops:
  0.6 4.3 %copy-start.6 = (s32[1,32]{1,0:T(1,128)S(1)}, s32[1,32]{1,0:T(1,128)}, u32[]{:S(2)}) copy-start(s32[1,32]{1,0:T(1,128)} %param.10) | copy-start | bytes 388
  0.6 4.9 %copy-start.2 = (bf16[1152,128]{1,0:T(8,128)(2,1)S(1)}, bf16[1152,128]{1,0:T(8,128)(2,1)}, u32[]{:S(2)}) copy-start(bf16[1152,128]{1,0:T(8,128)(2,1)} %param.12) | copy-start | bytes 884740
  2.0 5.6 %copy-start.3 = (bf16[512,256]{1,0:T(8,128)(2,1)S(1)}, bf16[512,256]{1,0:T(8,128)(2,1)}, u32[]{:S(2)}) copy-start(bf16[512,256]{1,0:T(8,128)(2,1)} %param.13) | copy-start | bytes 786436
  3.4 4.6 %copy-start.4 = (bf16[256,512]{1,0:T(8,128)(2,1)S(1)}, bf16[256,512]{1,0:T(8,128)(2,1)}, u32[]{:S(2)}) copy-start(bf16[256,512]{1,0:T(8,128)(2,1)} %param.14) | copy-start | bytes 786436
  3.5 9.6 %collective-permute-start = (bf16[2,32,16,256]{3,2,1,0:T(8,128)(2,1)S(1)}, bf16[2,32,16,256]{3,2,1,0:T(8,128)(2,1)}, u32[]{:S(2)}, u32[]{:S(2)}) collective-permute-start(bf16[2,32,16,256]{3,2,1,0:T(8,128)(2,1)S(1)} %constant_dynamic-update-slice_fusion), channel_id=1, source_target_pairs={{1,0},{2,1},{3,2},{4,3},{5,4},{6,5},{7,6},{0,7},{9,8},{10,9},{11,1... | collective-permute-start | bytes 1572872 | tf_op jit(solution)/shard_map/ppermute | solution.py:34
  6.0 2.4 %copy-start.5 = (bf16[128,128]{1,0:T(8,128)(2,1)S(1)}, bf16[128,128]{1,0:T(8,128)(2,1)}, u32[]{:S(2)}) copy-start(bf16[128,128]{1,0:T(8,128)(2,1)} %param.15) | copy-start | bytes 98308
  6.1 2.5 %copy-start.7 = (s32[1,32]{1,0:T(1,128)S(1)}, s32[1,32]{1,0:T(1,128)}, u32[]{:S(2)}) copy-start(s32[1,32]{1,0:T(1,128)} %param.11) | copy-start | bytes 388
  52.0 2.0 %collective-permute-start.1 = (bf16[2048,128]{1,0:T(8,128)(2,1)S(1)}, bf16[2048,128]{1,0:T(8,128)(2,1)S(1)}, u32[]{:S(2)}, u32[]{:S(2)}) collective-permute-start(bf16[2048,128]{1,0:T(8,128)(2,1)S(1)} %slice_bitcast_fusion), channel_id=1, source_target_pairs={{1,0},{0,1},{3,2},{2,3},{5,4},{4,5},{7,6},{6,7},{9,8},{8,9},{11,10... | collective-permute-start | bytes 1572872 | tf_op jit(solution)/shard_map/ppermute | solution.py:34
  55.9 24.7 %all-to-all-start = ((bf16[64,32,128]{2,1,0:T(8,128)(2,1)}), bf16[64,32,128]{2,1,0:T(8,128)(2,1)S(1)}, u32[]{:S(2)}, u32[]{:S(2)}) async-start(bf16[64,32,128]{2,1,0:T(8,128)(2,1)} %bitcast.33), calls=%async_computation | async-start | bytes 1048576 | tf_op jit(solution)/shard_map/all_to_all | solution.py:321
  80.7 9.1 %collective-permute-start.2 = (bf16[32,16,256]{2,1,0:T(8,128)(2,1)S(1)}, bf16[32,16,256]{2,1,0:T(8,128)(2,1)S(1)}, u32[]{:S(2)}, u32[]{:S(2)}) collective-permute-start(bf16[32,16,256]{2,1,0:T(8,128)(2,1)S(1)} %slice.112), channel_id=1, source_target_pairs={{7,0},{0,1},{1,2},{2,3},{3,4},{4,5},{5,6},{6,7},{15,8},{8,9},{9,10... | collective-permute-start | bytes 786440 | tf_op jit(solution)/shard_map/ppermute | solution.py:34
  83.5 19.6 %all-to-all-start.1 = ((bf16[64,32,128]{2,1,0:T(8,128)(2,1)}), bf16[64,32,128]{2,1,0:T(8,128)(2,1)S(1)}, u32[]{:S(2)}, u32[]{:S(2)}) async-start(bf16[64,32,128]{2,1,0:T(8,128)(2,1)} %broadcast_in_dim.37), calls=%async_computation.1 | async-start | bytes 1048576 | tf_op jit(solution)/shard_map/all_to_all | solution.py:328
  103.1 1.9 %copy-start = (bf16[64,32,128]{2,1,0:T(8,128)(2,1)}, bf16[64,32,128]{2,1,0:T(8,128)(2,1)S(1)}, u32[]{:S(2)}) copy-start(bf16[64,32,128]{2,1,0:T(8,128)(2,1)S(1)} %all-to-all-done.1) | copy-start | bytes 1572868
  103.1 1.9 %collective-permute-start.3 = (bf16[2048,128]{1,0:T(8,128)(2,1)S(1)}, bf16[2048,128]{1,0:T(8,128)(2,1)S(1)}, u32[]{:S(2)}, u32[]{:S(2)}) collective-permute-start(bf16[2048,128]{1,0:T(8,128)(2,1)S(1)} %bitcast.83), channel_id=1, source_target_pairs={{1,0},{0,1},{3,2},{2,3},{5,4},{4,5},{7,6},{6,7},{9,8},{8,9},{11,10... | collective-permute-start | bytes 1572872 | tf_op jit(solution)/shard_map/ppermute | solution.py:34
  105.0 0.8 copy-start.1

commit v4 on v3

--- a/solution.py
+++ b/solution.py
@@ -86,9 +86,9 @@
 
 def patch_kernel(
     count, parity, starts, alphas, betas,
-    feat, noise, w_in, w_dn, w_dn_t, w_u, w_u_t, w_o, w_o_t,
-    dpre_out, grads_out,
-    slots, first, slope, g_conv, g_down, g_up, g_out, loss,
+    own, right, far, w_in, w_dn, w_dn_t, w_u, w_u_t, w_o, w_o_t,
+    dpre_out, keep, send,
+    window, grads, slots, first, slope, g_conv, g_down, g_up, g_out, loss,
 ):
     g_conv[...] = jnp.zeros_like(g_conv)
     g_down[...] = jnp.zeros_like(g_down)
@@ -96,11 +96,15 @@
     g_out[...] = jnp.zeros_like(g_out)
     loss[...] = jnp.zeros_like(loss)
     zero_edges(slots)
+    core = parity[0]
+    for block, place in ((own, core), (right, core + 1), (far, 2 - 2 * core)):
+        for i in range(2):
+            window[i, pl.ds(place * SIDE, SIDE)] = block[i]
 
     def one_patch(k, carry):
         start = starts[k]
-        f = feat[pl.ds(start, SIDE)].reshape(CELLS, 2 * C).astype(f32)
-        e = noise[pl.ds(start, SIDE)].reshape(CELLS, 2 * C).astype(f32)
+        f = window[0, pl.ds(start, SIDE)].reshape(CELLS, 2 * C).astype(f32)
+        e = window[1, pl.ds(start, SIDE)].reshape(CELLS, 2 * C).astype(f32)
         fill_slots(slots, alphas[k] * f + betas[k] * e)
         pre = dot(taps(slots), w_in[...])
         sig = 0.5 * jnp.tanh(0.5 * pre) + 0.5
@@ -114,7 +118,7 @@
         slope2 = sig2 + act2 * (1.0 - sig2)
         coarse = act2.astype(bf16)
         up = dot(coarse, w_u[...])
-        ep = noise.at[pl.ds(start, SIDE)]
+        ep = window.at[1, pl.ds(start, SIDE)]
         merged = []
         dmerged = []
         derr = []
@@ -146,7 +150,7 @@
 
     def put(index, block):
         half = index // BLOCKS
-        grads_out[half ^ parity[0], pl.ds(index % BLOCKS * C, C)] = block.astype(bf16)
+        grads[half ^ core, pl.ds(index % BLOCKS * C, C)] = block.astype(bf16)
 
     for i in range(3):
         for j in range(3):
@@ -163,23 +167,28 @@
     put(26, jnp.concatenate([part, jnp.zeros((C - 8, C), f32)], axis=0))
     for index in range(27, 2 * BLOCKS):
         put(index, jnp.zeros((C, C), f32))
+    keep[...] = grads[0]
+    send[...] = grads[1]
 
 
 SLOPE = (HALF, 2, HALF, 2 * C)
 
 
-def input_kernel(count, starts, alphas, dpre, w_back, out, slots):
-    out[...] = jnp.zeros_like(out)
+def input_kernel(count, parity, starts, alphas, dpre, w_back, own, send, total, slots):
+    total[...] = jnp.zeros_like(total)
     zero_edges(slots)
 
     def one_patch(k, carry):
         fill_slots(slots, dpre[k].astype(f32))
         back = dot(taps(slots), w_back[...]) * alphas[k]
-        window = out.at[pl.ds(starts[k], SIDE)]
+        window = total.at[pl.ds(starts[k], SIDE)]
         window[...] += back.reshape(SIDE, HALF, 2 * C)
         return carry
 
     lax.fori_loop(0, count[0], one_patch, 0)
+    own[...] = total[pl.ds(parity[0] * SIDE, SIDE)]
+    send[0:SIDE] = total[pl.ds((1 - parity[0]) * SIDE, SIDE)].astype(bf16)
+    send[SIDE : 2 * SIDE] = total[2 * SIDE : 3 * SIDE].astype(bf16)
 
 
 def smem():
@@ -190,16 +199,19 @@
     return pl.BlockSpec(memory_space=pltpu.VMEM)
 
 
-def run_patches(count, parity, starts, alphas, betas, feat, noise, weights):
+def run_patches(count, parity, starts, alphas, betas, blocks, weights):
     return pl.pallas_call(
         patch_kernel,
         out_shape=(
             jax.ShapeDtypeStruct((PMAX, CELLS, 2 * C), bf16),
-            jax.ShapeDtypeStruct((2, BLOCKS * C, C), bf16),
+            jax.ShapeDtypeStruct((BLOCKS * C, C), bf16),
+            jax.ShapeDtypeStruct((BLOCKS * C, C), bf16),
         ),
-        in_specs=[smem()] * 5 + [vmem()] * 9,
-        out_specs=(vmem(), vmem()),
+        in_specs=[smem()] * 5 + [vmem()] * 10,
+        out_specs=(vmem(), vmem(), vmem()),
         scratch_shapes=[
+            pltpu.VMEM((2, 3 * SIDE, HALF, 2 * C), bf16),
+            pltpu.VMEM((2, BLOCKS * C, C), bf16),
             pltpu.VMEM((SIDE + 2, HALF, 4 * C), bf16),
             pltpu.VMEM(SLOPE, bf16),
             pltpu.VMEM(SLOPE, f32),
@@ -211,19 +223,25 @@
         ],
         compiler_params=pltpu.CompilerParams(vmem_limit_bytes=50 << 20),
         name="patches",
-    )(count, parity, starts, alphas, betas, feat, noise, *weights)
-
-
-def run_inputs(count, starts, alphas, dpre, w_back):
+    )(count, parity, starts, alphas, betas, *blocks, *weights)
+
+
+def run_inputs(count, parity, starts, alphas, dpre, w_back):
     return pl.pallas_call(
         input_kernel,
-        out_shape=jax.ShapeDtypeStruct((2 * SIDE, HALF, 2 * C), f32),
-        in_specs=[smem()] * 3 + [vmem()] * 2,
-        out_specs=vmem(),
-        scratch_shapes=[pltpu.VMEM((SIDE + 2, HALF, 4 * C), bf16)],
+        out_shape=(
+            jax.ShapeDtypeStruct((SIDE, HALF, 2 * C), f32),
+            jax.ShapeDtypeStruct((2 * SIDE, HALF, 2 * C), bf16),
+        ),
+        in_specs=[smem()] * 4 + [vmem()] * 2,
+        out_specs=(vmem(), vmem()),
+        scratch_shapes=[
+            pltpu.VMEM((3 * SIDE, HALF, 2 * C), f32),
+            pltpu.VMEM((SIDE + 2, HALF, 4 * C), bf16),
+        ],
         compiler_params=pltpu.CompilerParams(vmem_limit_bytes=50 << 20),
         name="inputs",
-    )(count, starts, alphas, dpre, w_back)
+    )(count, parity, starts, alphas, dpre, w_back)
 
 
 def run_finish(parity, half, other, cells):
@@ -293,36 +311,43 @@
 
 def per_device(encoder_features, noise, patch_cols, timesteps, w_conv, w_down, w_up, w_out):
     block_cols = encoder_features.shape[1]
-    lon_index = lax.axis_index(LON)
+    chip_index = lax.axis_index("x")
+    core = lax.axis_index("core")
     starts_all = patch_cols[0]
     band_patches = starts_all.shape[0]
 
     both = jnp.stack([pack_rows(encoder_features), pack_rows(noise)])
-    nxt = shifted(both, LON, -1)
-    window = jnp.concatenate([both, nxt], axis=1)
-
-    mine = (starts_all // block_cols) == lon_index
-    rank = jnp.cumsum(mine.astype(jnp.int32)) - 1
-    pick = mine[None, :] & (rank[None, :] == jnp.arange(PMAX, dtype=jnp.int32)[:, None])
-    starts = jnp.sum(jnp.where(pick, starts_all[None, :] - lon_index * block_cols, 0), axis=1)
+    right = shifted(both, LON, -1)
+    far = shifted(jnp.where(core == 0, both, right), "core", 1)
+
+    here = (starts_all // (2 * block_cols)) == chip_index
+    rank = jnp.cumsum(here.astype(jnp.int32)) - 1
+    mine = here & (rank % 2 == core)
+    pick = mine[None, :] & (rank[None, :] // 2 == jnp.arange(PMAX, dtype=jnp.int32)[:, None])
+    starts = jnp.sum(jnp.where(pick, starts_all[None, :] - chip_index * 2 * block_cols, 0), axis=1)
     levels = jnp.sum(jnp.where(pick, timesteps[0][None, :], 0), axis=1)
     count = jnp.sum(mine.astype(jnp.int32)).reshape(1)
-    parity = lax.axis_index("core").reshape(1)
+    parity = core.reshape(1)
     sigma = sigma_of(levels)
     alphas = 1.0 / jnp.sqrt(1.0 + sigma * sigma)
     betas = alphas * sigma
 
     weights, w_back = layout_weights(w_conv, w_down, w_up, w_out)
-    dpre, grads = run_patches(count, parity, starts, alphas, betas, window[0], window[1], weights)
-
-    theirs = shifted(grads[1], "core", 1)
-    chip = (grads[0].astype(f32) + theirs.astype(f32)).astype(bf16)
+    dpre, keep, send = run_patches(
+        count, parity, starts, alphas, betas, (both, right, far), weights
+    )
+
+    theirs = shifted(send, "core", 1)
+    chip = (keep.astype(f32) + theirs.astype(f32)).astype(bf16)
     chip, dpre = lax.optimization_barrier((chip, dpre))
     chunks = lax.all_to_all(chip.reshape(NCHIP, CHUNK, C), CHIPS, 0, 0, tiled=True)
-    grad_win = run_inputs(count, starts, alphas, dpre, w_back)
-    chunks, grad_win = lax.optimization_barrier((chunks, grad_win))
-    returned = shifted(grad_win[block_cols:].astype(bf16), LON, 1)
-    feature_grad = unpack_rows(grad_win[:block_cols] + returned.astype(f32))
+    own, give = run_inputs(count, parity, starts, alphas, dpre, w_back)
+    taken = shifted(give, "core", 1)
+    edge = (give[block_cols:].astype(f32) + taken[block_cols:].astype(f32)).astype(bf16)
+    size = lax.axis_size(LON)
+    returned = lax.ppermute(edge, LON, [(i, (i + 1) % size) for i in range(1, size, 2)])
+    chunks, own, taken, returned = lax.optimization_barrier((chunks, own, taken, returned))
+    feature_grad = unpack_rows(own + taken[:block_cols].astype(f32) + returned.astype(f32))
 
     total = jnp.sum(chunks.astype(f32), axis=0).astype(bf16)
     half = lax.all_to_all(

time: 109 us -> 101 us (0.927)
  Pallas kernels: 49 us -> 32.6 us
  starting transfers between devices: 22 us -> 27.3 us
  waiting for transfers between devices: 22.5 us -> 26.9 us
  other arithmetic: 4.44 us -> 2.45 us
    pallas_call x1, Pallas kernels: 36.7 us -> 23.1 us  [run_patches(): pl.pallas_call(patch_kernel, out_shape=(jax.ShapeDtypeStruct((PMAX, CELLS...]
    all_to_all x1, waiting for transfers between devices: 2.91 us -> 9.31 us  [per_device(): lax.all_to_all(chip.reshape(NCHIP, CHUNK, C), CHIPS, 0, 0, tiled=True)]
    ppermute x0 -> x1, starting transfers between devices: none -> 3.4 us  [per_device(): lax.ppermute(edge, LON, [(i, (i + 1) % size) for i in range(1, size, 2)])]
    pallas_call x1, Pallas kernels: 9.66 us -> 6.85 us  [run_inputs(): pl.pallas_call(input_kernel, out_shape=(jax.ShapeDtypeStruct((SIDE, HALF,...]
    ppermute x4 -> x5, starting transfers between devices: 3.66 us -> 6.19 us  [shifted(): return lax.ppermute(block, axis, route)]
    all_to_all x1, waiting for transfers between devices: 11.8 us -> 9.9 us  [per_device(): lax.all_to_all(jnp.broadcast_to(total[None], (NCHIP, CHUNK, C)), CHIPS, 0...]
    squeeze x1 -> x0, other arithmetic: 1.12 us -> none  [per_device(): window[1]]
    ppermute x4 -> x5, waiting for transfers between devices: 7.71 us -> 7.74 us  [shifted(): return lax.ppermute(block, axis, route)]
  transfers between devices with their start and end apart: 6 -> 8, of which waited for: 5 -> 6; matrix products, arithmetic and copies ran while one was open for 6% -> 6% of each run, Pallas kernels for 9% -> 0%
where the time goes in v4:
time: 101 us; the launch traced here: 99.7 us
  Pallas kernels  32.6 us (32%)
  starting transfers between devices  27.3 us (27%)
  waiting for transfers between devices  26.9 us (27%)
  local copies, waits for them, and re-layouts  9.23 us (9%)
  other arithmetic  2.45 us (2%)
  between operations  1.11 us (1%)
    pallas_call x1, Pallas kernels, run_patches(): pl.pallas_call(patch_kernel, out_shape=(jax.ShapeDtypeStruct((PMAX, CELLS...  23.1 us
    all_to_all x1, starting transfers between devices, per_device(): lax.all_to_all(chip.reshape(NCHIP, CHUNK, C), CHIPS, 0, 0, tiled=True)  12 us
    all_to_all x1, waiting for transfers between devices, per_device(): lax.all_to_all(jnp.broadcast_to(total[None], (NCHIP, CHUNK, C)), CHIPS, 0...  9.9 us
    all_to_all x1, waiting for transfers between devices, per_device(): lax.all_to_all(chip.reshape(NCHIP, CHUNK, C), CHIPS, 0, 0, tiled=True)  9.31 us
    ppermute x5, waiting for transfers between devices, shifted(): return lax.ppermute(block, axis, route)  7.74 us
    pallas_call x1, Pallas kernels, run_inputs(): pl.pallas_call(input_kernel, out_shape=(jax.ShapeDtypeStruct((SIDE, HALF,...  6.85 us
    ppermute x5, starting transfers between devices, shifted(): return lax.ppermute(block, axis, route)  6.19 us
    all_to_all x1, starting transfers between devices, per_device(): lax.all_to_all(jnp.broadcast_to(total[None], (NCHIP, CHUNK, C)), CHIPS, 0...  5.74 us
  transfers between devices with their start and end apart: 8, of which 6 were waited for; matrix products, arithmetic and copies ran while one was open for 6% of the time, Pallas kernels for 0%

profile of v4, /device:TPU:1, one launch (start us, length us, event | category | flops | bytes accessed | tf_op | source)
XLA Modules:
  0.0 99.7 jit_solution(9504444143055813410)
XLA Ops:
  0.7 1.2 %copy.83 = bf16[16,2,32,128]{3,1,0,2:T(2,128)(2,1)S(1)} copy(bf16[16,2,32,128]{3,2,1,0:T(8,128)(2,1)} %bitcast.121) | data formatting | bytes 524288 | tf_op jit(solution)/shard_map/reshape | solution.py:53
  1.9 0.2 stack_reshape.6
  2.1 1.2 %copy.82 = bf16[16,2,32,128]{3,1,0,2:T(2,128)(2,1)S(1)} copy(bf16[16,2,32,128]{3,2,1,0:T(8,128)(2,1)} %bitcast.122) | data formatting | bytes 524288 | tf_op jit(solution)/shard_map/reshape | solution.py:53
  3.3 0.2 stack_reshape.7
  3.5 1.4 %collective-permute-start = (bf16[2,32,16,256]{3,2,1,0:T(8,128)(2,1)S(1)}, bf16[2,32,16,256]{3,2,1,0:T(8,128)(2,1)S(1)}, u32[]{:S(2)}, u32[]{:S(2)}) collective-permute-start(bf16[2,32,16,256]{3,2,1,0:T(8,128)(2,1)S(1)} %constant_dynamic-update-slice_fusion.own), channel_id=1, source_target_pairs={{1,0},{2,1},{3,2},{4,3},{5,4},{6,5},{7,6},{0,7},{9,8},{10,9},{11,1... | collective-permute-start | bytes 1572872 | tf_op jit(solution)/shard_map/ppermute | solution.py:34
  5.2 0.2 copy.64
  5.5 0.1 copy.68.w_dn
  5.7 0.2 copy.65
  5.9 0.1 copy.69.w_u
  7.5 1.2 %copy.67.w_in = bf16[1536,256]{1,0:T(8,128)(2,1)} copy(bf16[1536,256]{0,1:T(8,128)(2,1)S(1)} %pad_dynamic-update-slice_fusion.6) | data formatting | bytes 1572864 | tf_op jit(solution)/shard_map/concatenate | solution.py:292
  8.9 0.6 and_select_fusion
  9.6 3.4 %collective-permute-done.right = bf16[2,32,16,256]{3,2,1,0:T(8,128)(2,1)S(1)} collective-permute-done((bf16[2,32,16,256]{3,2,1,0:T(8,128)(2,1)S(1)}, bf16[2,32,16,256]{3,2,1,0:T(8,128)(2,1)S(1)}, u32[]{:S(2)}, u32[]{:S(2)}) %collective-permute-start) | collective-permute-done | bytes 524320 | tf_op jit(solution)/shard_map/ppermute | solution.py:34
  13.0 1.0 %collective-permute-start.1 = (bf16[2,32,16,256]{3,2,1,0:T(8,128)(2,1)S(1)}, bf16[2,32,16,256]{3,2,1,0:T(8,128)(2,1)S(1)}, u32[]{:S(2)}, u32[]{:S(2)}) collective-permute-start(bf16[2,32,16,256]{3,2,1,0:T(8,128)(2,1)S(1)} %broadcast_select_fusion), channel_id=1, source_target_pairs={{1,0},{0,1},{3,2},{2,3},{5,4},{4,5},{7,6},{6,7},{9,8},{8,9},{11,10... | collective-permute-start | bytes 1572872 | tf_op jit(solution)/shard_map/ppermute | solution.py:34
  14.2 1.4 %collective-permute-done.1.far = bf16[2,32,16,256]{3,2,1,0:T(8,128)(2,1)S(1)} collective-permute-done((bf16[2,32,16,256]{3,2,1,0:T(8,128)(2,1)S(1)}, bf16[2,32,16,256]{3,2,1,0:T(8,128)(2,1)S(1)}, u32[]{:S(2)}, u32[]{:S(2)}) %collective-permute-start.1) | collective-permute-done | bytes 524320 | tf_op jit(solution)/shard_map/ppermute | solution.py:34
  15.6 23.1 %patches.1 = (bf16[12,512,256]{2,1,0:T(8,128)(2,1)}, bf16[2048,128]{1,0:T(8,128)(2,1)S(1)}, bf16[2048,128]{1,0:T(8,128)(2,1)S(1)}) custom-call(s32[1]{0:T(128)} %bitcast.2.count, s32[1]{0:T(128)} %bitcast.3.parity, s32[12]{0:T(128)S(1)} %get-tuple-element.43.starts, f32[12]{0:T(128)S(1)} %get-tuple-element.45.alphas, f32[12]{0:T(128)S(1)} %get-tuple-element.44.betas, ...), custom_call_target="tpu_custom_call" | custom-call | tf_op jit(solution)/shard_map/patches/pallas_call | solution.py:203
  38.7 0.4 collective-permute-start.2
  39.2 1.5 %collective-permute-done.2 = bf16[2048,128]{1,0:T(8,128)(2,1)S(1)} collective-permute-done((bf16[2048,128]{1,0:T(8,128)(2,1)S(1)}, bf16[2048,128]{1,0:T(8,128)(2,1)S(1)}, u32[]{:S(2)}, u32[]{:S(2)}) %collective-permute-start.2) | collective-permute-done | bytes 524320 | tf_op jit(solution)/shard_map/ppermute | solution.py:34
  40.6 0.9 add_convert_fusion
  41.6 6.8 %inputs.1 = (f32[32,16,256]{2,1,0:T(8,128)S(1)}, bf16[64,16,256]{2,1,0:T(8,128)(2,1)S(1)}) custom-call(s32[1]{0:T(128)} %bitcast.2.count, s32[1]{0:T(128)} %bitcast.3.parity, s32[12]{0:T(128)S(1)} %get-tuple-element.43.starts, f32[12]{0:T(128)S(1)} %get-tuple-element.45.alphas, bf16[12,512,256]{2,1,0:T(8,128)(2,1)} %get-tuple-element.28.dpre, ...), custom_call_target="tpu_custom_call" | custom-call | tf_op jit(solution)/shard_map/inputs/pallas_call | solution.py:230
  48.4 0.5 collective-permute-start.3
  48.9 12.0 %all-to-all-start = ((bf16[64,32,128]{2,1,0:T(8,128)(2,1)}), bf16[64,32,128]{2,1,0:T(8,128)(2,1)S(1)}, u32[]{:S(2)}, u32[]{:S(2)}) async-start(bf16[64,32,128]{2,1,0:T(8,128)(2,1)} %bitcast.29), calls=%async_computation | async-start | bytes 1048576 | tf_op jit(solution)/shard_map/all_to_all | solution.py:343
  61.0 3.4 %collective-permute-start.4 = (bf16[32,16,256]{2,1,0:T(8,128)(2,1)S(1)}, bf16[32,16,256]{2,1,0:T(8,128)(2,1)S(1)}, u32[]{:S(2)}, u32[]{:S(2)}) collective-permute-start(bf16[32,16,256]{2,1,0:T(8,128)(2,1)S(1)} %add_convert_fusion.1), channel_id=1, source_target_pairs={{1,2},{3,4},{5,6},{7,0},{9,10},{11,12},{13,14},{15,8},{17,18},{19,... | collective-permute-start | bytes 786440 | tf_op jit(solution)/shard_map/ppermute | solution.py:348
  64.4 9.3 %all-to-all-done = bf16[64,32,128]{2,1,0:T(8,128)(2,1)S(1)} async-done(((bf16[64,32,128]{2,1,0:T(8,128)(2,1)}), bf16[64,32,128]{2,1,0:T(8,128)(2,1)S(1)}, u32[]{:S(2)}, u32[]{:S(2)}) %all-to-all-start) | async-done | bytes 524320 | tf_op jit(solution)/shard_map/all_to_all | solution.py:343
  73.8 0.9 broadcast_in_dim.37
  74.6 5.7 %all-to-all-start.1 = ((bf16[64,32,128]{2,1,0:T(8,128)(2,1)}), bf16[64,32,128]{2,1,0:T(8,128)(2,1)S(1)}, u32[]{:S(2)}, u32[]{:S(2)}) async-start(bf16[64,32,128]{2,1,0:T(8,128)(2,1)} %broadcast_in_dim.37), calls=%async_computation.1 | async-start | bytes 1048576 | tf_op jit(solution)/shard_map/all_to_all | solution.py:353
  80.5 0.3 reshape.230
  80.8 1.1 %copy.70 = f32[16,2,32,128]{3,2,1,0:T(8,128)} copy(f32[16,2,32,128]{3,1,0,2:T(2,128)S(1)} %bitcast.79) | data formatting | bytes 1048576 | tf_op jit(solution)/shard_map/transpose | solution.py:60
  81.9 9.9 %all-to-all-done.1 = bf16[64,32,128]{2,1,0:T(8,128)(2,1)S(1)} async-done(((bf16[64,32,128]{2,1,0:T(8,128)(2,1)}), bf16[64,32,128]{2,1,0:T(8,128)(2,1)S(1)}, u32[]{:S(2)}, u32[]{:S(2)}) %all-to-all-start.1) | async-done | bytes 524320 | tf_op jit(solution)/shard_map/all_to_all | solution.py:353
  91.8 2.9 %collective-permute-start.5 = (bf16[2048,128]{1,0:T(8,128)(2,1)S(1)}, bf16[2048,128]{1,0:T(8,128)(2,1)S(1)}, u32[]{:S(2)}, u32[]{:S(2)}) collective-permute-start(bf16[2048,128]{1,0:T(8,128)(2,1)S(1)} %bitcast.77), channel_id=1, source_target_pairs={{1,0},{0,1},{3,2},{2,3},{5,4},{4,5},{7,6},{6,7},{9,8},{8,9},{11,10... | collective-permute-start | bytes 1572872 | tf_op jit(solution)/shard_map/ppermute | solution.py:34
  94.7 1.5 %collective-permute-done.5.theirs = bf16[2048,128]{1,0:T(8,128)(2,1)S(1)} collective-permute-done((bf16[2048,128]{1,0:T(8,128)(2,1)S(1)}, bf16[2048,128]{1,0:T(8,128)(2,1)S(1)}, u32[]{:S(2)}, u32[]{:S(2)}) %collective-permute-start.5) | collective-permute-done | bytes 524320 | tf_op jit(solution)/shard_map/ppermute | solution.py:34
  96.3 0.8 copy-done.1
  97.1 2.6 %finish.1 = (f32[1152,128]{1,0:T(8,128)}, f32[512,256]{1,0:T(8,128)}, f32[256,512]{1,0:T(8,128)}, f32[128,128]{1,0:T(8,128)}, f32[1]{0:T(128)}) custom-call(s32[1]{0:T(128)} %bitcast.3.parity, bf16[2048,128]{1,0:T(8,128)(2,1)} %bitcast.78, bf16[2048,128]{1,0:T(8,128)(2,1)} %copy-done.1), custom_call_target="tpu_custom_call" | custom-call | tf_op jit(solution)/shard_map/finish/pallas_call | solution.py:266
  (69 shorter events, 2.6 us)
Async XLA Ops:
  0.6 4.3 %copy-start.6 = (s32[1,32]{1,0:T(1,128)S(1)}, s32[1,32]{1,0:T(1,128)}, u32[]{:S(2)}) copy-start(s32[1,32]{1,0:T(1,128)} %param.10) | copy-start | bytes 388
  0.6 4.4 %copy-start.5 = (bf16[128,128]{1,0:T(8,128)(2,1)S(1)}, bf16[128,128]{1,0:T(8,128)(2,1)}, u32[]{:S(2)}) copy-start(bf16[128,128]{1,0:T(8,128)(2,1)} %param.15) | copy-start | bytes 98308
  0.7 4.6 %copy-start.3 = (bf16[512,256]{1,0:T(8,128)(2,1)S(1)}, bf16[512,256]{1,0:T(8,128)(2,1)}, u32[]{:S(2)}) copy-start(bf16[512,256]{1,0:T(8,128)(2,1)} %param.13) | copy-start | bytes 786436
  0.7 5.0 %copy-start.4 = (bf16[256,512]{1,0:T(8,128)(2,1)S(1)}, bf16[256,512]{1,0:T(8,128)(2,1)}, u32[]{:S(2)}) copy-start(bf16[256,512]{1,0:T(8,128)(2,1)} %param.14) | copy-start | bytes 786436
  0.7 5.4 %copy-start.2 = (bf16[1152,128]{1,0:T(8,128)(2,1)S(1)}, bf16[1152,128]{1,0:T(8,128)(2,1)}, u32[]{:S(2)}) copy-start(bf16[1152,128]{1,0:T(8,128)(2,1)} %param.12) | copy-start | bytes 884740
  3.5 9.5 %collective-permute-start = (bf16[2,32,16,256]{3,2,1,0:T(8,128)(2,1)S(1)}, bf16[2,32,16,256]{3,2,1,0:T(8,128)(2,1)S(1)}, u32[]{:S(2)}, u32[]{:S(2)}) collective-permute-start(bf16[2,32,16,256]{3,2,1,0:T(8,128)(2,1)S(1)} %constant_dynamic-update-slice_fusion.own), channel_id=1, source_target_pairs={{1,0},{2,1},{3,2},{4,3},{5,4},{6,5},{7,6},{0,7},{9,8},{10,9},{11,1... | collective-permute-start | bytes 1572872 | tf_op jit(solution)/shard_map/ppermute | solution.py:34
  6.0 8.0 %copy-start.7 = (s32[1,32]{1,0:T(1,128)S(1)}, s32[1,32]{1,0:T(1,128)}, u32[]{:S(2)}) copy-start(s32[1,32]{1,0:T(1,128)} %param.11) | copy-start | bytes 388
  13.0 2.6 %collective-permute-start.1 = (bf16[2,32,16,256]{3,2,1,0:T(8,128)(2,1)S(1)}, bf16[2,32,16,256]{3,2,1,0:T(8,128)(2,1)S(1)}, u32[]{:S(2)}, u32[]{:S(2)}) collective-permute-start(bf16[2,32,16,256]{3,2,1,0:T(8,128)(2,1)S(1)} %broadcast_select_fusion), channel_id=1, source_target_pairs={{1,0},{0,1},{3,2},{2,3},{5,4},{4,5},{7,6},{6,7},{9,8},{8,9},{11,10... | collective-permute-start | bytes 1572872 | tf_op jit(solution)/shard_map/ppermute | solution.py:34
  38.7 1.9 %collective-permute-start.2 = (bf16[2048,128]{1,0:T(8,128)(2,1)S(1)}, bf16[2048,128]{1,0:T(8,128)(2,1)S(1)}, u32[]{:S(2)}, u32[]{:S(2)}) collective-permute-start(bf16[2048,128]{1,0:T(8,128)(2,1)S(1)} %get-tuple-element.25), channel_id=1, source_target_pairs={{1,0},{0,1},{3,2},{2,3},{5,4},{4,5},{7,6},{6,7},{9,8},{8,9},{11,10... | collective-permute-start | bytes 1572872 | tf_op jit(solution)/shard_map/ppermute | solution.py:34
  48.4 12.5 %collective-permute-start.3 = (bf16[64,16,256]{2,1,0:T(8,128)(2,1)S(1)}, bf16[64,16,256]{2,1,0:T(8,128)(2,1)S(1)}, u32[]{:S(2)}, u32[]{:S(2)}) collective-permute-start(bf16[64,16,256]{2,1,0:T(8,128)(2,1)S(1)} %get-tuple-element.30), channel_id=1, source_target_pairs={{1,0},{0,1},{3,2},{2,3},{5,4},{4,5},{7,6},{6,7},{9,8},{8,9},{11,10... | collective-permute-start | bytes 1572872 | tf_op jit(solution)/shard_map/ppermute | solution.py:34
  48.9 24.8 %all-to-all-start = ((bf16[64,32,128]{2,1,0:T(8,128)(2,1)}), bf16[64,32,128]{2,1,0:T(8,128)(2,1)S(1)}, u32[]{:S(2)}, u32[]{:S(2)}) async-start(bf16[64,32,128]{2,1,0:T(8,128)(2,1)} %bitcast.29), calls=%async_computation | async-start | bytes 1048576 | tf_op jit(solution)/shard_map/all_to_all | solution.py:343
  61.0 12.7 %collective-permute-start.4 = (bf16[32,16,256]{2,1,0:T(8,128)(2,1)S(1)}, bf16[32,16,256]{2,1,0:T(8,128)(2,1)S(1)}, u32[]{:S(2)}, u32[]{:S(2)}) collective-permute-start(bf16[32,16,256]{2,1,0:T(8,128)(2,1)S(1)} %add_convert_fusion.1), channel_id=1, source_target_pairs={{1,2},{3,4},{5,6},{7,0},{9,10},{11,12},{13,14},{15,8},{17,18},{19,... | collective-permute-start | bytes 786440 | tf_op jit(solution)/shard_map/ppermute | solution.py:348
  74.6 17.1 %all-to-all-start.1 = ((bf16[64,32,128]{2,1,0:T(8,128)(2,1)}), bf16[64,32,128]{2,1,0:T(8,128)(2,1)S(1)}, u32[]{:S(2)}, u32[]{:S(2)}) async-start(bf16[64,32,128]{2,1,0:T(8,128)(2,1)} %broadcast_in_dim.37), calls=%async_computation.1 | async-start | bytes 1048576 | tf_op jit(solution)/shard_map/all_to_all | solution.py:353
  91.8 4.5 %copy-start = (bf16[64,32,128]{2,1,0:T(8,128)(2,1)}, bf16[64,32,128]{2,1,0:T(8,128)(2,1)S(1)}, u32[]{:S(2)}) copy-start(bf16[64,32,128]{2,1,0:T(8,128)(2,1)S(1)} %all-to-all-done.1) | copy-start | bytes 1572868
  91.8 4.5 %collective-permute-start.5 = (bf16[2048,128]{1,0:T(8,128)(2,1)S(1)}, bf16[2048,128]{1,0:T(8,128)(2,1)S(1)}, u32[]{:S(2)}, u32[]{:S(2)}) collective-permute-start(bf16[2048,128]{1,0:T(8,128)(2,1)S(1)} %bitcast.77), channel_id=1, source_target_pairs={{1,0},{0,1},{3,2},{2,3},{5,4},{4,5},{7,6},{6,7},{9,8},{8,9},{11,10... | collective-permute-start | bytes 1572872 | tf_op jit(solution)/shard_map/ppermute | solution.py:34
  96.3 0.8 copy-start.1

commit v5 on v4

--- a/solution.py
+++ b/solution.py
@@ -174,7 +174,7 @@
 SLOPE = (HALF, 2, HALF, 2 * C)
 
 
-def input_kernel(count, parity, starts, alphas, dpre, w_back, own, send, total, slots):
+def input_kernel(count, parity, starts, alphas, dpre, w_back, own, give, edge, total, slots):
     total[...] = jnp.zeros_like(total)
     zero_edges(slots)
 
@@ -187,8 +187,8 @@
 
     lax.fori_loop(0, count[0], one_patch, 0)
     own[...] = total[pl.ds(parity[0] * SIDE, SIDE)]
-    send[0:SIDE] = total[pl.ds((1 - parity[0]) * SIDE, SIDE)].astype(bf16)
-    send[SIDE : 2 * SIDE] = total[2 * SIDE : 3 * SIDE].astype(bf16)
+    give[...] = total[pl.ds((1 - parity[0]) * SIDE, SIDE)].astype(bf16)
+    edge[...] = total[2 * SIDE : 3 * SIDE].astype(bf16)
 
 
 def smem():
@@ -231,10 +231,11 @@
         input_kernel,
         out_shape=(
             jax.ShapeDtypeStruct((SIDE, HALF, 2 * C), f32),
-            jax.ShapeDtypeStruct((2 * SIDE, HALF, 2 * C), bf16),
+            jax.ShapeDtypeStruct((SIDE, HALF, 2 * C), bf16),
+            jax.ShapeDtypeStruct((SIDE, HALF, 2 * C), bf16),
         ),
         in_specs=[smem()] * 4 + [vmem()] * 2,
-        out_specs=(vmem(), vmem()),
+        out_specs=(vmem(), vmem(), vmem()),
         scratch_shapes=[
             pltpu.VMEM((3 * SIDE, HALF, 2 * C), f32),
             pltpu.VMEM((SIDE + 2, HALF, 4 * C), bf16),
@@ -341,13 +342,15 @@
     chip = (keep.astype(f32) + theirs.astype(f32)).astype(bf16)
     chip, dpre = lax.optimization_barrier((chip, dpre))
     chunks = lax.all_to_all(chip.reshape(NCHIP, CHUNK, C), CHIPS, 0, 0, tiled=True)
-    own, give = run_inputs(count, parity, starts, alphas, dpre, w_back)
+    own, give, edge = run_inputs(count, parity, starts, alphas, dpre, w_back)
+    chunks, own, give, edge = lax.optimization_barrier((chunks, own, give, edge))
     taken = shifted(give, "core", 1)
-    edge = (give[block_cols:].astype(f32) + taken[block_cols:].astype(f32)).astype(bf16)
     size = lax.axis_size(LON)
-    returned = lax.ppermute(edge, LON, [(i, (i + 1) % size) for i in range(1, size, 2)])
-    chunks, own, taken, returned = lax.optimization_barrier((chunks, own, taken, returned))
-    feature_grad = unpack_rows(own + taken[:block_cols].astype(f32) + returned.astype(f32))
+    near = lax.ppermute(edge, LON, [(i, (i + 1) % size) for i in range(1, size, 2)])
+    over = lax.ppermute(edge, LON, [(i, (i + 2) % size) for i in range(0, size, 2)])
+    feature_grad = unpack_rows(
+        own + taken.astype(f32) + (near.astype(f32) + over.astype(f32))
+    )
 
     total = jnp.sum(chunks.astype(f32), axis=0).astype(bf16)
     half = lax.all_to_all(

time: 101 us -> 99.5 us (0.985); the launches traced: 99.7 us -> 99.8 us
  Pallas kernels: 32.6 us -> 19.2 us
  starting transfers between devices: 27.3 us -> 40.7 us
    all_to_all x1, starting transfers between devices: 12 us -> 24.8 us  [per_device(): lax.all_to_all(chip.reshape(NCHIP, CHUNK, C), CHIPS, 0, 0, tiled=True)]
    pallas_call x1, Pallas kernels: 23.1 us -> 12 us  [run_patches(): pl.pallas_call(patch_kernel, out_shape=(jax.ShapeDtypeStruct((PMAX, CELLS...]
    pallas_call x1, Pallas kernels: 6.85 us -> 4.5 us  [run_inputs(): pl.pallas_call(input_kernel, out_shape=(jax.ShapeDtypeStruct((SIDE, HALF,...]
    all_to_all x1, waiting for transfers between devices: 9.31 us -> 7.82 us  [per_device(): lax.all_to_all(chip.reshape(NCHIP, CHUNK, C), CHIPS, 0, 0, tiled=True)]
    ppermute x5, starting transfers between devices: 6.19 us -> 4.73 us  [shifted(): return lax.ppermute(block, axis, route)]
    all_to_all x1, waiting for transfers between devices: 9.9 us -> 11.1 us  [per_device(): lax.all_to_all(jnp.broadcast_to(total[None], (NCHIP, CHUNK, C)), CHIPS, 0...]
  transfers between devices with their start and end apart: 8 -> 9, of which waited for: 6 -> 6; matrix products, arithmetic and copies ran while one was open for 6% -> 7% of each run, Pallas kernels for 0% -> 5%
where the time goes in v5:
time: 99.5 us; the launch traced here: 99.8 us
  starting transfers between devices  40.7 us (41%)
  waiting for transfers between devices  27.2 us (27%)
  Pallas kernels  19.2 us (19%)
  local copies, waits for them, and re-layouts  9.2 us (9%)
  other arithmetic  2.4 us (2%)
  between operations  1.13 us (1%)
    all_to_all x1, starting transfers between devices, per_device(): lax.all_to_all(chip.reshape(NCHIP, CHUNK, C), CHIPS, 0, 0, tiled=True)  24.8 us
    pallas_call x1, Pallas kernels, run_patches(): pl.pallas_call(patch_kernel, out_shape=(jax.ShapeDtypeStruct((PMAX, CELLS...  12 us
    all_to_all x1, waiting for transfers between devices, per_device(): lax.all_to_all(jnp.broadcast_to(total[None], (NCHIP, CHUNK, C)), CHIPS, 0...  11.1 us
    ppermute x5, waiting for transfers between devices, shifted(): return lax.ppermute(block, axis, route)  8.21 us
    all_to_all x1, waiting for transfers between devices, per_device(): lax.all_to_all(chip.reshape(NCHIP, CHUNK, C), CHIPS, 0, 0, tiled=True)  7.82 us
    all_to_all x1, starting transfers between devices, per_device(): lax.all_to_all(jnp.broadcast_to(total[None], (NCHIP, CHUNK, C)), CHIPS, 0...  6.66 us
    ppermute x5, starting transfers between devices, shifted(): return lax.ppermute(block, axis, route)  4.73 us
    pallas_call x1, Pallas kernels, run_inputs(): pl.pallas_call(input_kernel, out_shape=(jax.ShapeDtypeStruct((SIDE, HALF,...  4.5 us
  transfers between devices with their start and end apart: 9, of which 6 were waited for; matrix products, arithmetic and copies ran while one was open for 7% of the time, Pallas kernels for 5%

profile of v5, /device:TPU:1, one launch (start us, length us, event | category | flops | bytes accessed | tf_op | source)
XLA Modules:
  0.0 99.8 jit_solution(1292932451732812941)
XLA Ops:
  0.7 1.2 %copy.83 = bf16[16,2,32,128]{3,1,0,2:T(2,128)(2,1)S(1)} copy(bf16[16,2,32,128]{3,2,1,0:T(8,128)(2,1)} %bitcast.121) | data formatting | bytes 524288 | tf_op jit(solution)/shard_map/reshape | solution.py:53
  1.9 0.2 stack_reshape.6
  2.1 1.2 %copy.82 = bf16[16,2,32,128]{3,1,0,2:T(2,128)(2,1)S(1)} copy(bf16[16,2,32,128]{3,2,1,0:T(8,128)(2,1)} %bitcast.122) | data formatting | bytes 524288 | tf_op jit(solution)/shard_map/reshape | solution.py:53
  3.3 0.2 stack_reshape.7
  3.5 1.4 %collective-permute-start = (bf16[2,32,16,256]{3,2,1,0:T(8,128)(2,1)S(1)}, bf16[2,32,16,256]{3,2,1,0:T(8,128)(2,1)S(1)}, u32[]{:S(2)}, u32[]{:S(2)}) collective-permute-start(bf16[2,32,16,256]{3,2,1,0:T(8,128)(2,1)S(1)} %constant_dynamic-update-slice_fusion.own), channel_id=1, source_target_pairs={{1,0},{2,1},{3,2},{4,3},{5,4},{6,5},{7,6},{0,7},{9,8},{10,9},{11,1... | collective-permute-start | bytes 1572872 | tf_op jit(solution)/shard_map/ppermute | solution.py:34
  5.2 0.2 copy.64
  5.5 0.1 copy.68.w_dn
  5.7 0.2 copy.65
  5.9 0.1 copy.69.w_u
  7.5 1.2 %copy.67.w_in = bf16[1536,256]{1,0:T(8,128)(2,1)} copy(bf16[1536,256]{0,1:T(8,128)(2,1)S(1)} %pad_dynamic-update-slice_fusion.6) | data formatting | bytes 1572864 | tf_op jit(solution)/shard_map/concatenate | solution.py:293
  8.8 0.6 and_select_fusion
  9.5 3.5 %collective-permute-done.right = bf16[2,32,16,256]{3,2,1,0:T(8,128)(2,1)S(1)} collective-permute-done((bf16[2,32,16,256]{3,2,1,0:T(8,128)(2,1)S(1)}, bf16[2,32,16,256]{3,2,1,0:T(8,128)(2,1)S(1)}, u32[]{:S(2)}, u32[]{:S(2)}) %collective-permute-start) | collective-permute-done | bytes 524320 | tf_op jit(solution)/shard_map/ppermute | solution.py:34
  13.0 1.0 %collective-permute-start.1 = (bf16[2,32,16,256]{3,2,1,0:T(8,128)(2,1)S(1)}, bf16[2,32,16,256]{3,2,1,0:T(8,128)(2,1)S(1)}, u32[]{:S(2)}, u32[]{:S(2)}) collective-permute-start(bf16[2,32,16,256]{3,2,1,0:T(8,128)(2,1)S(1)} %broadcast_select_fusion), channel_id=1, source_target_pairs={{1,0},{0,1},{3,2},{2,3},{5,4},{4,5},{7,6},{6,7},{9,8},{8,9},{11,10... | collective-permute-start | bytes 1572872 | tf_op jit(solution)/shard_map/ppermute | solution.py:34
  14.2 1.4 %collective-permute-done.1.far = bf16[2,32,16,256]{3,2,1,0:T(8,128)(2,1)S(1)} collective-permute-done((bf16[2,32,16,256]{3,2,1,0:T(8,128)(2,1)S(1)}, bf16[2,32,16,256]{3,2,1,0:T(8,128)(2,1)S(1)}, u32[]{:S(2)}, u32[]{:S(2)}) %collective-permute-start.1) | collective-permute-done | bytes 524320 | tf_op jit(solution)/shard_map/ppermute | solution.py:34
  15.6 12.0 %patches.1 = (bf16[12,512,256]{2,1,0:T(8,128)(2,1)}, bf16[2048,128]{1,0:T(8,128)(2,1)S(1)}, bf16[2048,128]{1,0:T(8,128)(2,1)S(1)}) custom-call(s32[1]{0:T(128)} %bitcast.2.count, s32[1]{0:T(128)} %bitcast.3.parity, s32[12]{0:T(128)S(1)} %get-tuple-element.45.starts, f32[12]{0:T(128)S(1)} %get-tuple-element.47.alphas, f32[12]{0:T(128)S(1)} %get-tuple-element.46.betas, ...), custom_call_target="tpu_custom_call" | custom-call | tf_op jit(solution)/shard_map/patches/pallas_call | solution.py:203
  27.6 0.4 collective-permute-start.2
  28.1 1.5 %collective-permute-done.2 = bf16[2048,128]{1,0:T(8,128)(2,1)S(1)} collective-permute-done((bf16[2048,128]{1,0:T(8,128)(2,1)S(1)}, bf16[2048,128]{1,0:T(8,128)(2,1)S(1)}, u32[]{:S(2)}, u32[]{:S(2)}) %collective-permute-start.2) | collective-permute-done | bytes 524320 | tf_op jit(solution)/shard_map/ppermute | solution.py:34
  29.5 0.9 add_convert_fusion
  30.5 24.8 %all-to-all-start = ((bf16[64,32,128]{2,1,0:T(8,128)(2,1)}), bf16[64,32,128]{2,1,0:T(8,128)(2,1)S(1)}, u32[]{:S(2)}, u32[]{:S(2)}) async-start(bf16[64,32,128]{2,1,0:T(8,128)(2,1)} %bitcast.29), calls=%async_computation | async-start | bytes 1048576 | tf_op jit(solution)/shard_map/all_to_all | solution.py:344
  55.4 4.5 %inputs.1 = (f32[32,16,256]{2,1,0:T(8,128)S(1)}, bf16[32,16,256]{2,1,0:T(8,128)(2,1)S(1)}, bf16[32,16,256]{2,1,0:T(8,128)(2,1)S(1)}) custom-call(s32[1]{0:T(128)} %bitcast.2.count, s32[1]{0:T(128)} %bitcast.3.parity, s32[12]{0:T(128)S(1)} %get-tuple-element.45.starts, f32[12]{0:T(128)S(1)} %get-tuple-element.47.alphas, ...), custom_call_target="tpu_custom_call" | custom-call | tf_op jit(solution)/shard_map/inputs/pallas_call | solution.py:230
  59.9 7.8 %all-to-all-done = bf16[64,32,128]{2,1,0:T(8,128)(2,1)S(1)} async-done(((bf16[64,32,128]{2,1,0:T(8,128)(2,1)}), bf16[64,32,128]{2,1,0:T(8,128)(2,1)S(1)}, u32[]{:S(2)}, u32[]{:S(2)}) %all-to-all-start) | async-done | bytes 524320 | tf_op jit(solution)/shard_map/all_to_all | solution.py:344
  67.7 1.9 %collective-permute-start.3 = (bf16[32,16,256]{2,1,0:T(8,128)(2,1)S(1)}, bf16[32,16,256]{2,1,0:T(8,128)(2,1)S(1)}, u32[]{:S(2)}, u32[]{:S(2)}) collective-permute-start(bf16[32,16,256]{2,1,0:T(8,128)(2,1)S(1)} %get-tuple-element.35), channel_id=1, source_target_pairs={{1,0},{0,1},{3,2},{2,3},{5,4},{4,5},{7,6},{6,7},{9,8},{8,9},{11,10... | collective-permute-start | bytes 786440 | tf_op jit(solution)/shard_map/ppermute | solution.py:34
  69.6 0.7 collective-permute-start.5
  70.3 3.9 %collective-permute-start.4 = (bf16[32,16,256]{2,1,0:T(8,128)(2,1)S(1)}, bf16[32,16,256]{2,1,0:T(8,128)(2,1)S(1)}, u32[]{:S(2)}, u32[]{:S(2)}) collective-permute-start(bf16[32,16,256]{2,1,0:T(8,128)(2,1)S(1)} %get-tuple-element.36), channel_id=1, source_target_pairs={{1,2},{3,4},{5,6},{7,0},{9,10},{11,12},{13,14},{15,8},{17,18},{19,... | collective-permute-start | bytes 786440 | tf_op jit(solution)/shard_map/ppermute | solution.py:349
  74.3 0.9 broadcast_in_dim.37
  75.1 6.7 %all-to-all-start.1 = ((bf16[64,32,128]{2,1,0:T(8,128)(2,1)}), bf16[64,32,128]{2,1,0:T(8,128)(2,1)S(1)}, u32[]{:S(2)}, u32[]{:S(2)}) async-start(bf16[64,32,128]{2,1,0:T(8,128)(2,1)} %broadcast_in_dim.37), calls=%async_computation.1 | async-start | bytes 1048576 | tf_op jit(solution)/shard_map/all_to_all | solution.py:356
  82.0 0.3 reshape.230
  82.2 1.1 %copy.70 = f32[16,2,32,128]{3,2,1,0:T(8,128)} copy(f32[16,2,32,128]{3,1,0,2:T(2,128)S(1)} %bitcast.79) | data formatting | bytes 1048576 | tf_op jit(solution)/shard_map/transpose | solution.py:60
  83.3 11.1 %all-to-all-done.1 = bf16[64,32,128]{2,1,0:T(8,128)(2,1)S(1)} async-done(((bf16[64,32,128]{2,1,0:T(8,128)(2,1)}), bf16[64,32,128]{2,1,0:T(8,128)(2,1)S(1)}, u32[]{:S(2)}, u32[]{:S(2)}) %all-to-all-start.1) | async-done | bytes 524320 | tf_op jit(solution)/shard_map/all_to_all | solution.py:356
  94.5 1.9 %collective-permute-done.6.theirs = bf16[2048,128]{1,0:T(8,128)(2,1)S(1)} collective-permute-done((bf16[2048,128]{1,0:T(8,128)(2,1)S(1)}, bf16[2048,128]{1,0:T(8,128)(2,1)S(1)}, u32[]{:S(2)}, u32[]{:S(2)}) %collective-permute-start.6) | collective-permute-done | bytes 524320 | tf_op jit(solution)/shard_map/ppermute | solution.py:34
  96.4 0.8 copy-done.1
  97.2 2.6 %finish.1 = (f32[1152,128]{1,0:T(8,128)}, f32[512,256]{1,0:T(8,128)}, f32[256,512]{1,0:T(8,128)}, f32[128,128]{1,0:T(8,128)}, f32[1]{0:T(128)}) custom-call(s32[1]{0:T(128)} %bitcast.3.parity, bf16[2048,128]{1,0:T(8,128)(2,1)} %bitcast.78, bf16[2048,128]{1,0:T(8,128)(2,1)} %copy-done.1), custom_call_target="tpu_custom_call" | custom-call | tf_op jit(solution)/shard_map/finish/pallas_call | solution.py:267
  (70 shorter events, 2.5 us)
Async XLA Ops:
  0.6 4.3 %copy-start.6 = (s32[1,32]{1,0:T(1,128)S(1)}, s32[1,32]{1,0:T(1,128)}, u32[]{:S(2)}) copy-start(s32[1,32]{1,0:T(1,128)} %param.10) | copy-start | bytes 388
  0.6 4.4 %copy-start.5 = (bf16[128,128]{1,0:T(8,128)(2,1)S(1)}, bf16[128,128]{1,0:T(8,128)(2,1)}, u32[]{:S(2)}) copy-start(bf16[128,128]{1,0:T(8,128)(2,1)} %param.15) | copy-start | bytes 98308
  0.7 4.6 %copy-start.3 = (bf16[512,256]{1,0:T(8,128)(2,1)S(1)}, bf16[512,256]{1,0:T(8,128)(2,1)}, u32[]{:S(2)}) copy-start(bf16[512,256]{1,0:T(8,128)(2,1)} %param.13) | copy-start | bytes 786436
  0.7 5.0 %copy-start.4 = (bf16[256,512]{1,0:T(8,128)(2,1)S(1)}, bf16[256,512]{1,0:T(8,128)(2,1)}, u32[]{:S(2)}) copy-start(bf16[256,512]{1,0:T(8,128)(2,1)} %param.14) | copy-start | bytes 786436
  0.7 5.4 %copy-start.2 = (bf16[1152,128]{1,0:T(8,128)(2,1)S(1)}, bf16[1152,128]{1,0:T(8,128)(2,1)}, u32[]{:S(2)}) copy-start(bf16[1152,128]{1,0:T(8,128)(2,1)} %param.12) | copy-start | bytes 884740
  3.5 9.5 %collective-permute-start = (bf16[2,32,16,256]{3,2,1,0:T(8,128)(2,1)S(1)}, bf16[2,32,16,256]{3,2,1,0:T(8,128)(2,1)S(1)}, u32[]{:S(2)}, u32[]{:S(2)}) collective-permute-start(bf16[2,32,16,256]{3,2,1,0:T(8,128)(2,1)S(1)} %constant_dynamic-update-slice_fusion.own), channel_id=1, source_target_pairs={{1,0},{2,1},{3,2},{4,3},{5,4},{6,5},{7,6},{0,7},{9,8},{10,9},{11,1... | collective-permute-start | bytes 1572872 | tf_op jit(solution)/shard_map/ppermute | solution.py:34
  5.9 8.1 %copy-start.7 = (s32[1,32]{1,0:T(1,128)S(1)}, s32[1,32]{1,0:T(1,128)}, u32[]{:S(2)}) copy-start(s32[1,32]{1,0:T(1,128)} %param.11) | copy-start | bytes 388
  13.0 2.6 %collective-permute-start.1 = (bf16[2,32,16,256]{3,2,1,0:T(8,128)(2,1)S(1)}, bf16[2,32,16,256]{3,2,1,0:T(8,128)(2,1)S(1)}, u32[]{:S(2)}, u32[]{:S(2)}) collective-permute-start(bf16[2,32,16,256]{3,2,1,0:T(8,128)(2,1)S(1)} %broadcast_select_fusion), channel_id=1, source_target_pairs={{1,0},{0,1},{3,2},{2,3},{5,4},{4,5},{7,6},{6,7},{9,8},{8,9},{11,10... | collective-permute-start | bytes 1572872 | tf_op jit(solution)/shard_map/ppermute | solution.py:34
  27.6 1.9 %collective-permute-start.2 = (bf16[2048,128]{1,0:T(8,128)(2,1)S(1)}, bf16[2048,128]{1,0:T(8,128)(2,1)S(1)}, u32[]{:S(2)}, u32[]{:S(2)}) collective-permute-start(bf16[2048,128]{1,0:T(8,128)(2,1)S(1)} %get-tuple-element.26), channel_id=1, source_target_pairs={{1,0},{0,1},{3,2},{2,3},{5,4},{4,5},{7,6},{6,7},{9,8},{8,9},{11,10... | collective-permute-start | bytes 1572872 | tf_op jit(solution)/shard_map/ppermute | solution.py:34
  30.5 37.2 %all-to-all-start = ((bf16[64,32,128]{2,1,0:T(8,128)(2,1)}), bf16[64,32,128]{2,1,0:T(8,128)(2,1)S(1)}, u32[]{:S(2)}, u32[]{:S(2)}) async-start(bf16[64,32,128]{2,1,0:T(8,128)(2,1)} %bitcast.29), calls=%async_computation | async-start | bytes 1048576 | tf_op jit(solution)/shard_map/all_to_all | solution.py:344
  67.7 14.1 %collective-permute-start.3 = (bf16[32,16,256]{2,1,0:T(8,128)(2,1)S(1)}, bf16[32,16,256]{2,1,0:T(8,128)(2,1)S(1)}, u32[]{:S(2)}, u32[]{:S(2)}) collective-permute-start(bf16[32,16,256]{2,1,0:T(8,128)(2,1)S(1)} %get-tuple-element.35), channel_id=1, source_target_pairs={{1,0},{0,1},{3,2},{2,3},{5,4},{4,5},{7,6},{6,7},{9,8},{8,9},{11,10... | collective-permute-start | bytes 786440 | tf_op jit(solution)/shard_map/ppermute | solution.py:34
  69.6 12.2 %collective-permute-start.5 = (bf16[32,16,256]{2,1,0:T(8,128)(2,1)S(1)}, bf16[32,16,256]{2,1,0:T(8,128)(2,1)S(1)}, u32[]{:S(2)}, u32[]{:S(2)}) collective-permute-start(bf16[32,16,256]{2,1,0:T(8,128)(2,1)S(1)} %get-tuple-element.36), channel_id=1, source_target_pairs={{0,2},{2,4},{4,6},{6,0},{8,10},{10,12},{12,14},{14,8},{16,18},{18,... | collective-permute-start | bytes 786440 | tf_op jit(solution)/shard_map/ppermute | solution.py:350
  70.3 11.6 %collective-permute-start.4 = (bf16[32,16,256]{2,1,0:T(8,128)(2,1)S(1)}, bf16[32,16,256]{2,1,0:T(8,128)(2,1)S(1)}, u32[]{:S(2)}, u32[]{:S(2)}) collective-permute-start(bf16[32,16,256]{2,1,0:T(8,128)(2,1)S(1)} %get-tuple-element.36), channel_id=1, source_target_pairs={{1,2},{3,4},{5,6},{7,0},{9,10},{11,12},{13,14},{15,8},{17,18},{19,... | collective-permute-start | bytes 786440 | tf_op jit(solution)/shard_map/ppermute | solution.py:349
  75.1 19.3 %all-to-all-start.1 = ((bf16[64,32,128]{2,1,0:T(8,128)(2,1)}), bf16[64,32,128]{2,1,0:T(8,128)(2,1)S(1)}, u32[]{:S(2)}, u32[]{:S(2)}) async-start(bf16[64,32,128]{2,1,0:T(8,128)(2,1)} %broadcast_in_dim.37), calls=%async_computation.1 | async-start | bytes 1048576 | tf_op jit(solution)/shard_map/all_to_all | solution.py:356
  94.5 1.9 %copy-start = (bf16[64,32,128]{2,1,0:T(8,128)(2,1)}, bf16[64,32,128]{2,1,0:T(8,128)(2,1)S(1)}, u32[]{:S(2)}) copy-start(bf16[64,32,128]{2,1,0:T(8,128)(2,1)S(1)} %all-to-all-done.1) | copy-start | bytes 1572868
  94.5 1.9 %collective-permute-start.6 = (bf16[2048,128]{1,0:T(8,128)(2,1)S(1)}, bf16[2048,128]{1,0:T(8,128)(2,1)S(1)}, u32[]{:S(2)}, u32[]{:S(2)}) collective-permute-start(bf16[2048,128]{1,0:T(8,128)(2,1)S(1)} %bitcast.77), channel_id=1, source_target_pairs={{1,0},{0,1},{3,2},{2,3},{5,4},{4,5},{7,6},{6,7},{9,8},{8,9},{11,10... | collective-permute-start | bytes 1572872 | tf_op jit(solution)/shard_map/ppermute | solution.py:34
  96.4 0.8 copy-start.1

commit v6 on v5

--- a/solution.py
+++ b/solution.py
@@ -343,7 +343,7 @@
     chip, dpre = lax.optimization_barrier((chip, dpre))
     chunks = lax.all_to_all(chip.reshape(NCHIP, CHUNK, C), CHIPS, 0, 0, tiled=True)
     own, give, edge = run_inputs(count, parity, starts, alphas, dpre, w_back)
-    chunks, own, give, edge = lax.optimization_barrier((chunks, own, give, edge))
+    chunks, own = lax.optimization_barrier((chunks, own))
     taken = shifted(give, "core", 1)
     size = lax.axis_size(LON)
     near = lax.ppermute(edge, LON, [(i, (i + 1) % size) for i in range(1, size, 2)])

time: 99.5 us -> 98.3 us (0.988)
  waiting for transfers between devices: 27.2 us -> 19.6 us
  starting transfers between devices: 40.7 us -> 47.3 us
    all_to_all x1, waiting for transfers between devices: 7.82 us -> 0.01 us  [per_device(): lax.all_to_all(chip.reshape(NCHIP, CHUNK, C), CHIPS, 0, 0, tiled=True)]
    ppermute x1, starting transfers between devices: 3.9 us -> 8.75 us  [per_device(): lax.ppermute(edge, LON, [(i, (i + 1) % size) for i in range(1, size, 2)])]
    all_to_all x1, starting transfers between devices: 6.66 us -> 8.16 us  [per_device(): lax.all_to_all(jnp.broadcast_to(total[None], (NCHIP, CHUNK, C)), CHIPS, 0...]
  transfers between devices with their start and end apart: 9 -> 9, of which waited for: 6 -> 5; matrix products, arithmetic and copies ran while one was open for 7% -> 7% of each run, Pallas kernels for 5% -> 5%
where the time goes in v6:
time: 98.3 us; the launch traced here: 98.8 us
  starting transfers between devices  47.3 us (48%)
  waiting for transfers between devices  19.6 us (20%)
  Pallas kernels  19.2 us (20%)
  local copies, waits for them, and re-layouts  9.2 us (9%)
  other arithmetic  2.4 us (2%)
  between operations  1.13 us (1%)
    all_to_all x1, starting transfers between devices, per_device(): lax.all_to_all(chip.reshape(NCHIP, CHUNK, C), CHIPS, 0, 0, tiled=True)  25.1 us
    pallas_call x1, Pallas kernels, run_patches(): pl.pallas_call(patch_kernel, out_shape=(jax.ShapeDtypeStruct((PMAX, CELLS...  12 us
    all_to_all x1, waiting for transfers between devices, per_device(): lax.all_to_all(jnp.broadcast_to(total[None], (NCHIP, CHUNK, C)), CHIPS, 0...  11.8 us
    ppermute x1, starting transfers between devices, per_device(): lax.ppermute(edge, LON, [(i, (i + 1) % size) for i in range(1, size, 2)])  8.75 us
    all_to_all x1, starting transfers between devices, per_device(): lax.all_to_all(jnp.broadcast_to(total[None], (NCHIP, CHUNK, C)), CHIPS, 0...  8.16 us
    ppermute x5, waiting for transfers between devices, shifted(): return lax.ppermute(block, axis, route)  7.84 us
    ppermute x5, starting transfers between devices, shifted(): return lax.ppermute(block, axis, route)  4.56 us
    pallas_call x1, Pallas kernels, run_inputs(): pl.pallas_call(input_kernel, out_shape=(jax.ShapeDtypeStruct((SIDE, HALF,...  4.5 us
  transfers between devices with their start and end apart: 9, of which 5 were waited for; matrix products, arithmetic and copies ran while one was open for 7% of the time, Pallas kernels for 5%

profile of v6, /device:TPU:1, one launch (start us, length us, event | category | flops | bytes accessed | tf_op | source)
XLA Modules:
  0.0 98.8 jit_solution(7406194735560737821)
XLA Ops:
  0.7 1.2 %copy.83 = bf16[16,2,32,128]{3,1,0,2:T(2,128)(2,1)S(1)} copy(bf16[16,2,32,128]{3,2,1,0:T(8,128)(2,1)} %bitcast.121) | data formatting | bytes 524288 | tf_op jit(solution)/shard_map/reshape | solution.py:53
  1.9 0.2 stack_reshape.6
  2.1 1.2 %copy.82 = bf16[16,2,32,128]{3,1,0,2:T(2,128)(2,1)S(1)} copy(bf16[16,2,32,128]{3,2,1,0:T(8,128)(2,1)} %bitcast.122) | data formatting | bytes 524288 | tf_op jit(solution)/shard_map/reshape | solution.py:53
  3.3 0.2 stack_reshape.7
  3.5 1.4 %collective-permute-start = (bf16[2,32,16,256]{3,2,1,0:T(8,128)(2,1)S(1)}, bf16[2,32,16,256]{3,2,1,0:T(8,128)(2,1)S(1)}, u32[]{:S(2)}, u32[]{:S(2)}) collective-permute-start(bf16[2,32,16,256]{3,2,1,0:T(8,128)(2,1)S(1)} %constant_dynamic-update-slice_fusion.own), channel_id=1, source_target_pairs={{1,0},{2,1},{3,2},{4,3},{5,4},{6,5},{7,6},{0,7},{9,8},{10,9},{11,1... | collective-permute-start | bytes 1572872 | tf_op jit(solution)/shard_map/ppermute | solution.py:34
  5.2 0.2 copy.64
  5.5 0.1 copy.68.w_dn
  5.7 0.2 copy.65
  5.9 0.1 copy.69.w_u
  7.5 1.2 %copy.67.w_in = bf16[1536,256]{1,0:T(8,128)(2,1)} copy(bf16[1536,256]{0,1:T(8,128)(2,1)S(1)} %pad_dynamic-update-slice_fusion.6) | data formatting | bytes 1572864 | tf_op jit(solution)/shard_map/concatenate | solution.py:293
  8.8 0.6 and_select_fusion
  9.5 3.5 %collective-permute-done.right = bf16[2,32,16,256]{3,2,1,0:T(8,128)(2,1)S(1)} collective-permute-done((bf16[2,32,16,256]{3,2,1,0:T(8,128)(2,1)S(1)}, bf16[2,32,16,256]{3,2,1,0:T(8,128)(2,1)S(1)}, u32[]{:S(2)}, u32[]{:S(2)}) %collective-permute-start) | collective-permute-done | bytes 524320 | tf_op jit(solution)/shard_map/ppermute | solution.py:34
  13.0 1.0 %collective-permute-start.1 = (bf16[2,32,16,256]{3,2,1,0:T(8,128)(2,1)S(1)}, bf16[2,32,16,256]{3,2,1,0:T(8,128)(2,1)S(1)}, u32[]{:S(2)}, u32[]{:S(2)}) collective-permute-start(bf16[2,32,16,256]{3,2,1,0:T(8,128)(2,1)S(1)} %broadcast_select_fusion), channel_id=1, source_target_pairs={{1,0},{0,1},{3,2},{2,3},{5,4},{4,5},{7,6},{6,7},{9,8},{8,9},{11,10... | collective-permute-start | bytes 1572872 | tf_op jit(solution)/shard_map/ppermute | solution.py:34
  14.2 1.4 %collective-permute-done.1.far = bf16[2,32,16,256]{3,2,1,0:T(8,128)(2,1)S(1)} collective-permute-done((bf16[2,32,16,256]{3,2,1,0:T(8,128)(2,1)S(1)}, bf16[2,32,16,256]{3,2,1,0:T(8,128)(2,1)S(1)}, u32[]{:S(2)}, u32[]{:S(2)}) %collective-permute-start.1) | collective-permute-done | bytes 524320 | tf_op jit(solution)/shard_map/ppermute | solution.py:34
  15.6 12.0 %patches.1 = (bf16[12,512,256]{2,1,0:T(8,128)(2,1)}, bf16[2048,128]{1,0:T(8,128)(2,1)S(1)}, bf16[2048,128]{1,0:T(8,128)(2,1)S(1)}) custom-call(s32[1]{0:T(128)} %bitcast.2.count, s32[1]{0:T(128)} %bitcast.3.parity, s32[12]{0:T(128)S(1)} %get-tuple-element.41.starts, f32[12]{0:T(128)S(1)} %get-tuple-element.43.alphas, f32[12]{0:T(128)S(1)} %get-tuple-element.42.betas, ...), custom_call_target="tpu_custom_call" | custom-call | tf_op jit(solution)/shard_map/patches/pallas_call | solution.py:203
  27.6 0.4 collective-permute-start.2
  28.1 1.5 %collective-permute-done.2 = bf16[2048,128]{1,0:T(8,128)(2,1)S(1)} collective-permute-done((bf16[2048,128]{1,0:T(8,128)(2,1)S(1)}, bf16[2048,128]{1,0:T(8,128)(2,1)S(1)}, u32[]{:S(2)}, u32[]{:S(2)}) %collective-permute-start.2) | collective-permute-done | bytes 524320 | tf_op jit(solution)/shard_map/ppermute | solution.py:34
  29.5 0.9 add_convert_fusion
  30.5 25.1 %all-to-all-start = ((bf16[64,32,128]{2,1,0:T(8,128)(2,1)}), bf16[64,32,128]{2,1,0:T(8,128)(2,1)S(1)}, u32[]{:S(2)}, u32[]{:S(2)}) async-start(bf16[64,32,128]{2,1,0:T(8,128)(2,1)} %bitcast.29), calls=%async_computation | async-start | bytes 1048576 | tf_op jit(solution)/shard_map/all_to_all | solution.py:344
  55.7 4.5 %inputs.1 = (f32[32,16,256]{2,1,0:T(8,128)S(1)}, bf16[32,16,256]{2,1,0:T(8,128)(2,1)S(1)}, bf16[32,16,256]{2,1,0:T(8,128)(2,1)S(1)}) custom-call(s32[1]{0:T(128)} %bitcast.2.count, s32[1]{0:T(128)} %bitcast.3.parity, s32[12]{0:T(128)S(1)} %get-tuple-element.41.starts, f32[12]{0:T(128)S(1)} %get-tuple-element.43.alphas, ...), custom_call_target="tpu_custom_call" | custom-call | tf_op jit(solution)/shard_map/inputs/pallas_call | solution.py:230
  60.2 0.7 collective-permute-start.3
  60.9 0.7 collective-permute-start.5
  61.6 8.8 %collective-permute-start.4 = (bf16[32,16,256]{2,1,0:T(8,128)(2,1)S(1)}, bf16[32,16,256]{2,1,0:T(8,128)(2,1)S(1)}, u32[]{:S(2)}, u32[]{:S(2)}) collective-permute-start(bf16[32,16,256]{2,1,0:T(8,128)(2,1)S(1)} %get-tuple-element.32), channel_id=1, source_target_pairs={{1,2},{3,4},{5,6},{7,0},{9,10},{11,12},{13,14},{15,8},{17,18},{19,... | collective-permute-start | bytes 786440 | tf_op jit(solution)/shard_map/ppermute | solution.py:349
  70.5 0.9 broadcast_in_dim.37
  71.3 8.2 %all-to-all-start.1 = ((bf16[64,32,128]{2,1,0:T(8,128)(2,1)}), bf16[64,32,128]{2,1,0:T(8,128)(2,1)S(1)}, u32[]{:S(2)}, u32[]{:S(2)}) async-start(bf16[64,32,128]{2,1,0:T(8,128)(2,1)} %broadcast_in_dim.37), calls=%async_computation.1 | async-start | bytes 1048576 | tf_op jit(solution)/shard_map/all_to_all | solution.py:356
  79.7 0.3 reshape.230
  80.0 1.1 %copy.70 = f32[16,2,32,128]{3,2,1,0:T(8,128)} copy(f32[16,2,32,128]{3,1,0,2:T(2,128)S(1)} %bitcast.79) | data formatting | bytes 1048576 | tf_op jit(solution)/shard_map/transpose | solution.py:60
  81.1 11.8 %all-to-all-done.1 = bf16[64,32,128]{2,1,0:T(8,128)(2,1)S(1)} async-done(((bf16[64,32,128]{2,1,0:T(8,128)(2,1)}), bf16[64,32,128]{2,1,0:T(8,128)(2,1)S(1)}, u32[]{:S(2)}, u32[]{:S(2)}) %all-to-all-start.1) | async-done | bytes 524320 | tf_op jit(solution)/shard_map/all_to_all | solution.py:356
  92.8 1.0 %collective-permute-start.6 = (bf16[2048,128]{1,0:T(8,128)(2,1)S(1)}, bf16[2048,128]{1,0:T(8,128)(2,1)S(1)}, u32[]{:S(2)}, u32[]{:S(2)}) collective-permute-start(bf16[2048,128]{1,0:T(8,128)(2,1)S(1)} %bitcast.77), channel_id=1, source_target_pairs={{1,0},{0,1},{3,2},{2,3},{5,4},{4,5},{7,6},{6,7},{9,8},{8,9},{11,10... | collective-permute-start | bytes 1572872 | tf_op jit(solution)/shard_map/ppermute | solution.py:34
  93.8 1.5 %collective-permute-done.6.theirs = bf16[2048,128]{1,0:T(8,128)(2,1)S(1)} collective-permute-done((bf16[2048,128]{1,0:T(8,128)(2,1)S(1)}, bf16[2048,128]{1,0:T(8,128)(2,1)S(1)}, u32[]{:S(2)}, u32[]{:S(2)}) %collective-permute-start.6) | collective-permute-done | bytes 524320 | tf_op jit(solution)/shard_map/ppermute | solution.py:34
  95.4 0.8 copy-done.1
  96.2 2.6 %finish.1 = (f32[1152,128]{1,0:T(8,128)}, f32[512,256]{1,0:T(8,128)}, f32[256,512]{1,0:T(8,128)}, f32[128,128]{1,0:T(8,128)}, f32[1]{0:T(128)}) custom-call(s32[1]{0:T(128)} %bitcast.3.parity, bf16[2048,128]{1,0:T(8,128)(2,1)} %bitcast.78, bf16[2048,128]{1,0:T(8,128)(2,1)} %copy-done.1), custom_call_target="tpu_custom_call" | custom-call | tf_op jit(solution)/shard_map/finish/pallas_call | solution.py:267
  (70 shorter events, 2.5 us)
Async XLA Ops:
  0.6 4.3 %copy-start.6 = (s32[1,32]{1,0:T(1,128)S(1)}, s32[1,32]{1,0:T(1,128)}, u32[]{:S(2)}) copy-start(s32[1,32]{1,0:T(1,128)} %param.10) | copy-start | bytes 388
  0.6 4.4 %copy-start.5 = (bf16[128,128]{1,0:T(8,128)(2,1)S(1)}, bf16[128,128]{1,0:T(8,128)(2,1)}, u32[]{:S(2)}) copy-start(bf16[128,128]{1,0:T(8,128)(2,1)} %param.15) | copy-start | bytes 98308
  0.7 4.6 %copy-start.3 = (bf16[512,256]{1,0:T(8,128)(2,1)S(1)}, bf16[512,256]{1,0:T(8,128)(2,1)}, u32[]{:S(2)}) copy-start(bf16[512,256]{1,0:T(8,128)(2,1)} %param.13) | copy-start | bytes 786436
  0.7 5.0 %copy-start.4 = (bf16[256,512]{1,0:T(8,128)(2,1)S(1)}, bf16[256,512]{1,0:T(8,128)(2,1)}, u32[]{:S(2)}) copy-start(bf16[256,512]{1,0:T(8,128)(2,1)} %param.14) | copy-start | bytes 786436
  0.7 5.4 %copy-start.2 = (bf16[1152,128]{1,0:T(8,128)(2,1)S(1)}, bf16[1152,128]{1,0:T(8,128)(2,1)}, u32[]{:S(2)}) copy-start(bf16[1152,128]{1,0:T(8,128)(2,1)} %param.12) | copy-start | bytes 884740
  3.5 9.5 %collective-permute-start = (bf16[2,32,16,256]{3,2,1,0:T(8,128)(2,1)S(1)}, bf16[2,32,16,256]{3,2,1,0:T(8,128)(2,1)S(1)}, u32[]{:S(2)}, u32[]{:S(2)}) collective-permute-start(bf16[2,32,16,256]{3,2,1,0:T(8,128)(2,1)S(1)} %constant_dynamic-update-slice_fusion.own), channel_id=1, source_target_pairs={{1,0},{2,1},{3,2},{4,3},{5,4},{6,5},{7,6},{0,7},{9,8},{10,9},{11,1... | collective-permute-start | bytes 1572872 | tf_op jit(solution)/shard_map/ppermute | solution.py:34
  5.9 8.1 %copy-start.7 = (s32[1,32]{1,0:T(1,128)S(1)}, s32[1,32]{1,0:T(1,128)}, u32[]{:S(2)}) copy-start(s32[1,32]{1,0:T(1,128)} %param.11) | copy-start | bytes 388
  13.0 2.6 %collective-permute-start.1 = (bf16[2,32,16,256]{3,2,1,0:T(8,128)(2,1)S(1)}, bf16[2,32,16,256]{3,2,1,0:T(8,128)(2,1)S(1)}, u32[]{:S(2)}, u32[]{:S(2)}) collective-permute-start(bf16[2,32,16,256]{3,2,1,0:T(8,128)(2,1)S(1)} %broadcast_select_fusion), channel_id=1, source_target_pairs={{1,0},{0,1},{3,2},{2,3},{5,4},{4,5},{7,6},{6,7},{9,8},{8,9},{11,10... | collective-permute-start | bytes 1572872 | tf_op jit(solution)/shard_map/ppermute | solution.py:34
  27.6 1.9 %collective-permute-start.2 = (bf16[2048,128]{1,0:T(8,128)(2,1)S(1)}, bf16[2048,128]{1,0:T(8,128)(2,1)S(1)}, u32[]{:S(2)}, u32[]{:S(2)}) collective-permute-start(bf16[2048,128]{1,0:T(8,128)(2,1)S(1)} %get-tuple-element.24), channel_id=1, source_target_pairs={{1,0},{0,1},{3,2},{2,3},{5,4},{4,5},{7,6},{6,7},{9,8},{8,9},{11,10... | collective-permute-start | bytes 1572872 | tf_op jit(solution)/shard_map/ppermute | solution.py:34
  30.5 39.9 %all-to-all-start = ((bf16[64,32,128]{2,1,0:T(8,128)(2,1)}), bf16[64,32,128]{2,1,0:T(8,128)(2,1)S(1)}, u32[]{:S(2)}, u32[]{:S(2)}) async-start(bf16[64,32,128]{2,1,0:T(8,128)(2,1)} %bitcast.29), calls=%async_computation | async-start | bytes 1048576 | tf_op jit(solution)/shard_map/all_to_all | solution.py:344
  60.2 19.3 %collective-permute-start.3 = (bf16[32,16,256]{2,1,0:T(8,128)(2,1)S(1)}, bf16[32,16,256]{2,1,0:T(8,128)(2,1)S(1)}, u32[]{:S(2)}, u32[]{:S(2)}) collective-permute-start(bf16[32,16,256]{2,1,0:T(8,128)(2,1)S(1)} %get-tuple-element.31), channel_id=1, source_target_pairs={{1,0},{0,1},{3,2},{2,3},{5,4},{4,5},{7,6},{6,7},{9,8},{8,9},{11,10... | collective-permute-start | bytes 786440 | tf_op jit(solution)/shard_map/ppermute | solution.py:34
  60.9 18.6 %collective-permute-start.5 = (bf16[32,16,256]{2,1,0:T(8,128)(2,1)S(1)}, bf16[32,16,256]{2,1,0:T(8,128)(2,1)S(1)}, u32[]{:S(2)}, u32[]{:S(2)}) collective-permute-start(bf16[32,16,256]{2,1,0:T(8,128)(2,1)S(1)} %get-tuple-element.32), channel_id=1, source_target_pairs={{0,2},{2,4},{4,6},{6,0},{8,10},{10,12},{12,14},{14,8},{16,18},{18,... | collective-permute-start | bytes 786440 | tf_op jit(solution)/shard_map/ppermute | solution.py:350
  61.6 17.9 %collective-permute-start.4 = (bf16[32,16,256]{2,1,0:T(8,128)(2,1)S(1)}, bf16[32,16,256]{2,1,0:T(8,128)(2,1)S(1)}, u32[]{:S(2)}, u32[]{:S(2)}) collective-permute-start(bf16[32,16,256]{2,1,0:T(8,128)(2,1)S(1)} %get-tuple-element.32), channel_id=1, source_target_pairs={{1,2},{3,4},{5,6},{7,0},{9,10},{11,12},{13,14},{15,8},{17,18},{19,... | collective-permute-start | bytes 786440 | tf_op jit(solution)/shard_map/ppermute | solution.py:349
  71.3 21.5 %all-to-all-start.1 = ((bf16[64,32,128]{2,1,0:T(8,128)(2,1)}), bf16[64,32,128]{2,1,0:T(8,128)(2,1)S(1)}, u32[]{:S(2)}, u32[]{:S(2)}) async-start(bf16[64,32,128]{2,1,0:T(8,128)(2,1)} %broadcast_in_dim.37), calls=%async_computation.1 | async-start | bytes 1048576 | tf_op jit(solution)/shard_map/all_to_all | solution.py:356
  92.8 2.5 %copy-start = (bf16[64,32,128]{2,1,0:T(8,128)(2,1)}, bf16[64,32,128]{2,1,0:T(8,128)(2,1)S(1)}, u32[]{:S(2)}) copy-start(bf16[64,32,128]{2,1,0:T(8,128)(2,1)S(1)} %all-to-all-done.1) | copy-start | bytes 1572868
  92.8 2.5 %collective-permute-start.6 = (bf16[2048,128]{1,0:T(8,128)(2,1)S(1)}, bf16[2048,128]{1,0:T(8,128)(2,1)S(1)}, u32[]{:S(2)}, u32[]{:S(2)}) collective-permute-start(bf16[2048,128]{1,0:T(8,128)(2,1)S(1)} %bitcast.77), channel_id=1, source_target_pairs={{1,0},{0,1},{3,2},{2,3},{5,4},{4,5},{7,6},{6,7},{9,8},{8,9},{11,10... | collective-permute-start | bytes 1572872 | tf_op jit(solution)/shard_map/ppermute | solution.py:34
  95.4 0.8 copy-start.1
